TPU v7x, 32 devices: a whole 2x2x4 slice. The times are simulated.
32 devices in a mesh: ctx: 8 (over y, x, core), tp: 4 (over z).
Axes of the slice: x: 2, y: 2, z: 4, core: 2. Of those that a mesh axis runs over, the one named last changes fastest.
Arguments:
- tokens: bfloat16 [4096, 4096], P('ctx', 'tp'), may hold values from -6 to 6
- norm_gain: float32 [4096], replicated, may hold values from 0.5 to 1.5
- proj_weight: bfloat16 [3, 4096, 2048], P(None, None, 'tp'), may hold values from -0.09375 to 0.09375
- short_taps: float32 [3, 3, 2048], P(None, None, 'tp'), may hold values from -1 to 1
- long_filter: float32 [4096, 2048], P('ctx', 'tp'), may hold values from -0.09375 to 0.09375
- skip_gain: float32 [2048], P('tp'), may hold values from -1 to 1
Outputs:
- output: bfloat16 [4096, 2048], P('ctx', 'tp')
All inputs are finite; a program needn't handle non-finite values.
Results may differ from a plain program's by a relative error of at most 0.0081.
Values may be sent and summed in bfloat16 or wider, within the bound.
A program may use at most 128 MiB of HBM per device.

v0:
```python
import math

import jax
import jax.numpy as jnp
from jax import lax
from jax.sharding import PartitionSpec as P

highest = lax.Precision.HIGHEST


def from_behind(array, axis, by):
    devices = lax.axis_size(axis)
    pairs = [(i, i + by) for i in range(devices) if 0 <= i + by < devices]
    return lax.ppermute(array, axis, pairs)


def outer_tables(part_count):
    frequency = jnp.arange(2 * part_count, dtype=jnp.int32)
    source = jnp.arange(part_count, dtype=jnp.int32)
    turn_count = frequency[:, None] * source[None, :] % (2 * part_count)
    angles = turn_count.astype(jnp.float32) * (math.pi / part_count)
    return (jnp.cos(angles), jnp.sin(angles))


def inner_tables(row_count):
    step_index = jnp.arange(row_count, dtype=jnp.int32)
    turn_count = step_index[:, None] * step_index[None, :] % row_count
    angles = turn_count.astype(jnp.float32) * (2.0 * math.pi / row_count)
    return (jnp.cos(angles), jnp.sin(angles))


def twist_tables(own_index, part_count, block_rows, total_length):
    frequency = jnp.arange(2 * part_count, dtype=jnp.int32)
    column = own_index * block_rows + jnp.arange(block_rows, dtype=jnp.int32)
    turn_count = frequency[:, None] * column[None, :] % total_length
    angles = turn_count.astype(jnp.float32) * (2.0 * math.pi / total_length)
    return (jnp.cos(angles)[:, :, None], jnp.sin(angles)[:, :, None])


def forward_transform(signal, part_count, tables, regroup, spread):
    outer_cos, outer_sin, inner_cos, inner_sin, twist_cos, twist_sin = tables
    row_count, width_all = signal.shape
    block_rows = row_count // part_count
    regrouped = regroup(signal).reshape(part_count, block_rows, width_all)
    outer_real = jnp.einsum("an,njw->ajw", outer_cos, regrouped, precision=highest)
    outer_imag = -jnp.einsum("an,njw->ajw", outer_sin, regrouped, precision=highest)
    turned_real = outer_real * twist_cos + outer_imag * twist_sin
    turned_imag = outer_imag * twist_cos - outer_real * twist_sin
    arrived = spread(jnp.stack([turned_real, turned_imag]))
    spec_real = jnp.einsum("bj,ejw->ebw", inner_cos, arrived[0], precision=highest) + jnp.einsum(
        "bj,ejw->ebw", inner_sin, arrived[1], precision=highest
    )
    spec_imag = jnp.einsum("bj,ejw->ebw", inner_cos, arrived[1], precision=highest) - jnp.einsum(
        "bj,ejw->ebw", inner_sin, arrived[0], precision=highest
    )
    return (spec_real, spec_imag)


def inverse_transform(spec_real, spec_imag, part_count, tables):
    outer_cos, outer_sin, inner_cos, inner_sin, twist_cos, twist_sin = tables
    row_count = spec_real.shape[1]
    width_all = spec_real.shape[2]
    back_real = jnp.einsum("jb,ebw->ejw", inner_cos, spec_real, precision=highest) - jnp.einsum(
        "jb,ebw->ejw", inner_sin, spec_imag, precision=highest
    )
    back_imag = jnp.einsum("jb,ebw->ejw", inner_sin, spec_real, precision=highest) + jnp.einsum(
        "jb,ebw->ejw", inner_cos, spec_imag, precision=highest
    )
    arrived = lax.all_to_all(
        jnp.stack([back_real, back_imag]), "ctx", split_axis=2, concat_axis=1, tiled=True
    )
    turned_real = arrived[0] * twist_cos - arrived[1] * twist_sin
    turned_imag = arrived[0] * twist_sin + arrived[1] * twist_cos
    total_length = 2 * row_count * part_count
    folded = (
        jnp.einsum("an,ajw->njw", outer_cos, turned_real, precision=highest)
        - jnp.einsum("an,ajw->njw", outer_sin, turned_imag, precision=highest)
    ) / total_length
    return lax.all_to_all(
        folded.reshape(row_count, width_all), "ctx", split_axis=0, concat_axis=0, tiled=True
    )


def body(tokens, norm_gain, proj_weight, short_taps, long_filter, skip_gain):
    gathered = lax.all_gather(tokens, "tp", axis=1, tiled=True)
    widened = gathered.astype(jnp.float32)
    scaling = lax.rsqrt(jnp.mean(widened * widened, axis=1, keepdims=True) + 1e-06)
    normed = (widened * scaling * norm_gain).astype(jnp.bfloat16)
    projected = jnp.einsum(
        "td,bdc->btc", normed, proj_weight, preferred_element_type=jnp.float32
    ).astype(jnp.bfloat16)
    previous = from_behind(projected[:, -2:, :], "ctx", 1)
    extended = jnp.concatenate([previous, projected], axis=1).astype(jnp.float32)
    branch = (
        short_taps[:, 0, None, :] * extended[:, 2:, :]
        + short_taps[:, 1, None, :] * extended[:, 1:-1, :]
        + short_taps[:, 2, None, :] * extended[:, :-2, :]
    )
    mixed_field = branch[1] * branch[2]
    row_count, channels = mixed_field.shape
    part_count = lax.axis_size("ctx")
    own_index = lax.axis_index("ctx")
    block_rows = row_count // part_count
    total_length = 2 * row_count * part_count
    outer_cos, outer_sin = outer_tables(part_count)
    inner_cos, inner_sin = inner_tables(row_count)
    twist_cos, twist_sin = twist_tables(own_index, part_count, block_rows, total_length)
    tables = (outer_cos, outer_sin, inner_cos, inner_sin, twist_cos, twist_sin)
    gain_real, gain_imag = forward_transform(
        long_filter,
        part_count,
        tables,
        lambda values: lax.all_to_all(values, "ctx", split_axis=0, concat_axis=0, tiled=True),
        lambda values: lax.all_to_all(
            values.astype(jnp.bfloat16), "ctx", split_axis=1, concat_axis=2, tiled=True
        ).astype(values.dtype),
    )
    data_real, data_imag = forward_transform(
        mixed_field,
        part_count,
        tables,
        lambda values: lax.all_to_all(values, "ctx", split_axis=0, concat_axis=0, tiled=True),
        lambda values: lax.all_to_all(
            values.astype(jnp.bfloat16), "ctx", split_axis=1, concat_axis=2, tiled=True
        ).astype(values.dtype),
    )
    product_real = data_real * gain_real - data_imag * gain_imag
    product_imag = data_real * gain_imag + data_imag * gain_real
    convolved = inverse_transform(product_real, product_imag, part_count, tables)
    return (branch[0] * (convolved + skip_gain * mixed_field)).astype(jnp.bfloat16)


def solution(mesh):
    placed = (
        P("ctx", "tp"),
        P(),
        P(None, None, "tp"),
        P(None, None, "tp"),
        P("ctx", "tp"),
        P("tp"),
    )
    return jax.shard_map(
        body, mesh=mesh, in_specs=placed, out_specs=P("ctx", "tp"), check_vma=False
    )
```

profile of v0, /device:TPU:0, one launch (start us, length us, event | category | flops | bytes accessed | tf_op | source)
XLA Modules:
  0.0 390.0 jit_solution(1918648023505237398)
XLA Ops:
  6.5 0.7 all-gather.2.cloned.1.call-update
  7.3 5.2 %all-to-all-start.2 = ((f32[8,64,512]{2,1,0:T(8,128)}), f32[8,64,512]{2,1,0:T(8,128)}, u32[]{:S(2)}, u32[]{:S(2)}) async-start(f32[8,64,512]{2,1,0:T(8,128)} %bitcast.138), calls=%async_computation.2 | async-start | bytes 2097152 | tf_op jit(solution)/shard_map/all_to_all | solution.py:113
  12.5 79.9 %all-gather.2.cloned.1.call-done = bf16[512,4096]{1,0:T(8,128)(2,1)} async-done(((bf16[512,1024]{1,0:T(8,128)(2,1)}), bf16[512,4096]{1,0:T(8,128)(2,1)}) %all-gather.2.cloned.1.call-update) | async-done | bytes 4194320 | tf_op jit(solution)/shard_map/all_gather | solution.py:85
  92.4 3.2 fusion
  95.9 9.9 %fusion.33 = bf16[3,512,512]{2,1,0:T(8,128)(2,1)S(1)} fusion(bf16[3,4096,512]{2,1,0:T(8,128)(2,1)} %param.8, bf16[512,4096]{1,0:T(8,128)(2,1)S(1)} %copy-done.3, f32[4096]{0:T(1024)S(1)} %copy-done.8, f32[512]{0:T(512)S(1)} %add_rsqrt_fusion), kind=kOutput, calls=%fused_computation.50 | convolution fusion | flops 6451625984 | bytes 18368512 | tf_op jit(solution)/shard_map/td,bdc->btc/dot_general | solution.py:89
  105.8 1.8 collective-permute-start
  107.6 0.8 collective-permute-done
  108.8 0.9 fusion.8
  109.8 1.2 slice_multiply_fusion.3
  110.9 6.3 %all-to-all-start = ((f32[8,64,512]{2,1,0:T(8,128)}), f32[8,64,512]{2,1,0:T(8,128)}, u32[]{:S(2)}, u32[]{:S(2)}) async-start(f32[8,64,512]{2,1,0:T(8,128)} %bitcast.135), calls=%async_computation | async-start | bytes 2097152 | tf_op jit(solution)/shard_map/all_to_all | solution.py:122
  117.4 4.7 %fusion.75 = f32[16,64,512]{2,0,1:T(8,128)} fusion(f32[8,64,512]{2,1,0:T(8,128)} %all-to-all-done.2), kind=kOutput, calls=%fused_computation.89 | convolution fusion | flops 50333440 | bytes 3145728 | tf_op jit(solution)/shard_map/an,njw->ajw/dot_general | solution.py:46
  122.2 4.8 %fusion.77 = f32[16,64,512]{2,0,1:T(8,128)} fusion(f32[8,64,512]{2,1,0:T(8,128)} %all-to-all-done.2), kind=kOutput, calls=%fused_computation.91 | convolution fusion | flops 50333440 | bytes 3145728 | tf_op jit(solution)/shard_map/an,njw->ajw/dot_general | solution.py:45
  126.9 5.7 %all-to-all-done = f32[8,64,512]{2,1,0:T(8,128)} async-done(((f32[8,64,512]{2,1,0:T(8,128)}), f32[8,64,512]{2,1,0:T(8,128)}, u32[]{:S(2)}, u32[]{:S(2)}) %all-to-all-start) | async-done | bytes 1048608 | tf_op jit(solution)/shard_map/all_to_all | solution.py:122
  132.7 3.6 fusion.79
  136.3 5.9 %fusion.47 = (bf16[1,16,64,512]{3,1,2,0:T(8,128)(2,1)S(1)}, bf16[1,16,64,512]{3,1,2,0:T(8,128)(2,1)S(1)}, bf16[1,16,64,512]{3,1,2,0:T(8,128)(2,1)}, bf16[1,16,64,512]{3,1,2,0:T(8,128)(2,1)}) fusion(f32[16,64,512]{2,0,1:T(8,128)S(1)} %copy-done.2, f32[16,64,512]{2,0,1:T(8,128)} %fusion.77, f32[16,64]{0,1:T(8,128)S(1)} %get-tuple-element.23, ...), kind=kOutput, calls=%fused_computation.58 | convolution fusion | flops 59770624 | bytes 11542528 | tf_op jit(solution)/shard_map/an,njw->ajw/dot_general | solution.py:45
  142.3 2.5 copy.59
  144.9 4.3 %all-to-all-start.3 = ((bf16[2,16,64,512]{3,2,0,1:T(8,128)(2,1)}), bf16[2,16,64,512]{3,2,0,1:T(8,128)(2,1)}, u32[]{:S(2)}, u32[]{:S(2)}) async-start(bf16[2,16,64,512]{3,2,0,1:T(8,128)(2,1)} %copy.59), calls=%async_computation.3 | async-start | bytes 4194304 | tf_op jit(solution)/shard_map/all_to_all | solution.py:114
  149.2 1.7 pad_maximum_fusion.1
  151.0 2.5 copy.51
  153.4 22.4 %all-to-all-done.3 = bf16[2,16,64,512]{3,2,0,1:T(8,128)(2,1)} async-done(((bf16[2,16,64,512]{3,2,0,1:T(8,128)(2,1)}), bf16[2,16,64,512]{3,2,0,1:T(8,128)(2,1)}, u32[]{:S(2)}, u32[]{:S(2)}) %all-to-all-start.3) | async-done | bytes 2097184 | tf_op jit(solution)/shard_map/all_to_all | solution.py:114
  175.9 4.6 %all-to-all-start.1 = ((bf16[2,16,64,512]{3,2,0,1:T(8,128)(2,1)}), bf16[2,16,64,512]{3,2,0,1:T(8,128)(2,1)}, u32[]{:S(2)}, u32[]{:S(2)}) async-start(bf16[2,16,64,512]{3,2,0,1:T(8,128)(2,1)} %copy.51), calls=%async_computation.1 | async-start | bytes 4194304 | tf_op jit(solution)/shard_map/all_to_all | solution.py:123
  180.5 1.8 copy.60
  182.7 6.9 %fusion.64 = f32[2,512,512]{2,1,0:T(8,128)S(1)} fusion(bf16[2,512,512]{2,1,0:T(8,128)(2,1)S(1)} %bitcast.141), kind=kOutput, calls=%fused_computation.78 | convolution fusion | flops 3224895488 | bytes 3145728 | tf_op jit(solution)/shard_map/bj,ejw->ebw/dot_general | solution.py:50
  189.6 6.9 %fusion.60 = f32[2,512,512]{2,1,0:T(8,128)S(1)} fusion(bf16[2,512,512]{2,1,0:T(8,128)(2,1)S(1)} %bitcast.139), kind=kOutput, calls=%fused_computation.74 | convolution fusion | flops 3224895488 | bytes 3145728 | tf_op jit(solution)/shard_map/bj,ejw->ebw/dot_general | solution.py:53
  196.5 7.4 %convolution_add_fusion = f32[2,512,512]{2,1,0:T(8,128)} fusion(f32[2,512,512]{2,1,0:T(8,128)S(1)} %fusion.64, bf16[2,512,512]{2,1,0:T(8,128)(2,1)S(1)} %bitcast.140), kind=kOutput, calls=%fused_computation.44 | convolution fusion | flops 3225419776 | bytes 5242880 | tf_op jit(solution)/shard_map/bj,ejw->ebw/dot_general | solution.py:50
  203.9 7.8 %convolution_subtract_fusion = f32[2,512,512]{2,1,0:T(8,128)} fusion(f32[2,512,512]{2,1,0:T(8,128)S(1)} %fusion.60, bf16[2,512,512]{2,1,0:T(8,128)(2,1)S(1)} %bitcast.142), kind=kOutput, calls=%fused_computation.42 | convolution fusion | flops 3225419776 | bytes 5242880 | tf_op jit(solution)/shard_map/bj,ejw->ebw/dot_general | solution.py:53
  211.7 1.8 copy.52
  213.9 6.9 %fusion.62 = f32[2,512,512]{2,1,0:T(8,128)S(1)} fusion(bf16[2,512,512]{2,1,0:T(8,128)(2,1)S(1)} %bitcast.143), kind=kOutput, calls=%fused_computation.76 | convolution fusion | flops 3224895488 | bytes 3145728 | tf_op jit(solution)/shard_map/bj,ejw->ebw/dot_general | solution.py:53
  220.9 6.9 %fusion.66 = f32[2,512,512]{2,1,0:T(8,128)S(1)} fusion(bf16[2,512,512]{2,1,0:T(8,128)(2,1)S(1)} %bitcast.136), kind=kOutput, calls=%fused_computation.80 | convolution fusion | flops 3224895488 | bytes 3145728 | tf_op jit(solution)/shard_map/bj,ejw->ebw/dot_general | solution.py:50
  227.8 7.2 %convolution_add_fusion.1 = f32[2,512,512]{2,1,0:T(8,128)S(1)} fusion(f32[2,512,512]{2,1,0:T(8,128)S(1)} %fusion.66, bf16[2,512,512]{2,1,0:T(8,128)(2,1)S(1)} %bitcast.144), kind=kOutput, calls=%fused_computation.45 | convolution fusion | flops 3225419776 | bytes 5242880 | tf_op jit(solution)/shard_map/bj,ejw->ebw/dot_general | solution.py:50
  235.0 7.5 %multiply_subtract_fusion = (f32[2,512,512]{2,1,0:T(8,128)S(1)}, f32[2,512,512]{2,1,0:T(8,128)S(1)}) fusion(f32[2,512,512]{2,1,0:T(8,128)S(1)} %copy-done.5, f32[2,512,512]{2,1,0:T(8,128)S(1)} %convolution_add_fusion.1, f32[2,512,512]{2,1,0:T(8,128)S(1)} %copy-done.4, f32[2,512,512]{2,1,0:T(8,128)S(1)} %fusion.62, bf16[2,512,512]{2,1,0:T(8,128)(2,1)S(1)} %bitcast.137), kind=kOutput, calls=%fused_computation.36 | convolution fusion | flops 3228565504 | bytes 13631488 | tf_op jit(solution)/shard_map/bj,ejw->ebw/dot_general | solution.py:53
  242.5 8.4 %fusion.10 = f32[2,512,512]{2,1,0:T(8,128)S(1)} fusion(f32[2,512,512]{2,1,0:T(8,128)S(1)} %get-tuple-element.6), kind=kOutput, calls=%fused_computation.17 | convolution fusion | flops 3224895488 | bytes 4194304 | tf_op jit(solution)/shard_map/jb,ebw->ejw/dot_general | solution.py:66
  250.9 8.6 %fusion.12 = f32[2,512,512]{2,1,0:T(8,128)S(1)} fusion(f32[2,512,512]{2,1,0:T(8,128)S(1)} %get-tuple-element.6), kind=kOutput, calls=%fused_computation.19 | convolution fusion | flops 3224895488 | bytes 4194304 | tf_op jit(solution)/shard_map/jb,ebw->ejw/dot_general | solution.py:63
  259.5 8.5 %subtract_bitcast_fusion = f32[1,2,512,512]{2,3,1,0:T(8,128)S(1)} fusion(f32[2,512,512]{2,1,0:T(8,128)S(1)} %fusion.12, f32[2,512,512]{2,1,0:T(8,128)S(1)} %get-tuple-element.5), kind=kOutput, calls=%fused_computation.34 | convolution fusion | flops 3225419776 | bytes 6291456 | tf_op jit(solution)/shard_map/jb,ebw->ejw/dot_general | solution.py:63
  268.0 8.5 %add_bitcast_fusion = f32[1,2,512,512]{2,3,1,0:T(8,128)S(1)} fusion(f32[2,512,512]{2,1,0:T(8,128)S(1)} %fusion.10, f32[2,512,512]{2,1,0:T(8,128)S(1)} %get-tuple-element.5), kind=kOutput, calls=%fused_computation.33 | convolution fusion | flops 3225419776 | bytes 6291456 | tf_op jit(solution)/shard_map/jb,ebw->ejw/dot_general | solution.py:66
  276.5 2.4 pad_maximum_fusion
  278.9 7.3 %copy.69 = f32[2,2,512,512]{3,1,0,2:T(2,128)} copy(f32[2,2,512,512]{2,3,1,0:T(8,128)} %pad_maximum_fusion) | data formatting | bytes 8388608 | tf_op jit(solution)/shard_map/stack | solution.py:70
  286.2 53.4 %all_to_all.69 = f32[2,2,512,512]{3,1,0,2:T(2,128)S(1)} all-to-all(f32[2,2,512,512]{3,1,0,2:T(2,128)} %copy.69), channel_id=1, replica_groups=mesh['ctx'=8,'tp'=4] {'ctx'}, dimensions={2} | all-to-all | bytes 8388608 | tf_op jit(solution)/shard_map/all_to_all | solution.py:69
  339.6 1.3 copy.70
  341.0 2.0 fusion.197
  342.9 3.0 copy.71
  345.9 3.6 squeeze.34
  349.6 4.6 %copy.72 = f32[1,8,2,64,512]{4,2,1,3,0:T(2,128)} copy(f32[1,8,2,64,512]{4,3,1,2,0:T(8,128)} %get-tuple-element.12) | data formatting | bytes 4194304 | tf_op jit(solution)/shard_map/slice | solution.py:72
  354.1 3.6 squeeze.35
  357.8 3.7 fusion.18
  361.5 1.4 fusion.39
  363.6 17.8 %all_to_all.70 = f32[8,64,512]{2,1,0:T(8,128)S(1)} all-to-all(f32[8,64,512]{2,1,0:T(8,128)S(1)} %copy.73), channel_id=1, replica_groups=mesh['ctx'=8,'tp'=4] {'ctx'}, dimensions={0} | all-to-all | bytes 2097152 | tf_op jit(solution)/shard_map/all_to_all | solution.py:79
  381.4 1.3 fusion.50
  (37 shorter events, 2.5 us)
Async XLA Ops:
  6.5 5.9 %copy-start.6 = (f32[3,3,512]{2,1,0:T(4,128)S(1)}, f32[3,3,512]{2,1,0:T(4,128)}, u32[]{:S(2)}) copy-start(f32[3,3,512]{2,1,0:T(4,128)} %param.9) | copy-start | bytes 55300
  6.5 85.9 %all-gather.2.cloned.1.call-start = ((), (), s32[]{:S(2)}) async-start(), calls=%async_computation.6 | async-start | bytes 5242880 | tf_op jit(solution)/shard_map/all_gather | solution.py:85
  7.3 103.7 %all-to-all-start.2 = ((f32[8,64,512]{2,1,0:T(8,128)}), f32[8,64,512]{2,1,0:T(8,128)}, u32[]{:S(2)}, u32[]{:S(2)}) async-start(f32[8,64,512]{2,1,0:T(8,128)} %bitcast.138), calls=%async_computation.2 | async-start | bytes 2097152 | tf_op jit(solution)/shard_map/all_to_all | solution.py:113
  12.4 83.2 %copy-start.8 = (f32[4096]{0:T(1024)S(1)}, f32[4096]{0:T(1024)}, u32[]{:S(2)}) copy-start(f32[4096]{0:T(1024)} %param.7) | copy-start | bytes 49156
  92.4 3.4 copy-start.3
  105.8 2.6 collective-permute-start
  110.9 21.7 %all-to-all-start = ((f32[8,64,512]{2,1,0:T(8,128)}), f32[8,64,512]{2,1,0:T(8,128)}, u32[]{:S(2)}, u32[]{:S(2)}) async-start(f32[8,64,512]{2,1,0:T(8,128)} %bitcast.135), calls=%async_computation | async-start | bytes 2097152 | tf_op jit(solution)/shard_map/all_to_all | solution.py:122
  132.7 3.6 copy-start.2
  144.9 31.0 %all-to-all-start.3 = ((bf16[2,16,64,512]{3,2,0,1:T(8,128)(2,1)}), bf16[2,16,64,512]{3,2,0,1:T(8,128)(2,1)}, u32[]{:S(2)}, u32[]{:S(2)}) async-start(bf16[2,16,64,512]{3,2,0,1:T(8,128)(2,1)} %copy.59), calls=%async_computation.3 | async-start | bytes 4194304 | tf_op jit(solution)/shard_map/all_to_all | solution.py:114
  175.9 35.9 %all-to-all-start.1 = ((bf16[2,16,64,512]{3,2,0,1:T(8,128)(2,1)}), bf16[2,16,64,512]{3,2,0,1:T(8,128)(2,1)}, u32[]{:S(2)}, u32[]{:S(2)}) async-start(bf16[2,16,64,512]{3,2,0,1:T(8,128)(2,1)} %copy.51), calls=%async_computation.1 | async-start | bytes 4194304 | tf_op jit(solution)/shard_map/all_to_all | solution.py:123
  227.8 7.2 %copy-start.4 = (f32[2,512,512]{2,1,0:T(8,128)S(1)}, f32[2,512,512]{2,1,0:T(8,128)}, u32[]{:S(2)}) copy-start(f32[2,512,512]{2,1,0:T(8,128)} %convolution_add_fusion) | copy-start | bytes 6291460
  227.8 7.2 %copy-start.5 = (f32[2,512,512]{2,1,0:T(8,128)S(1)}, f32[2,512,512]{2,1,0:T(8,128)}, u32[]{:S(2)}) copy-start(f32[2,512,512]{2,1,0:T(8,128)} %convolution_subtract_fusion) | copy-start | bytes 6291460
  357.8 3.8 copy-start
  357.8 3.8 copy-start.1
  363.0 18.4 %copy-start.7 = (f32[512]{0:T(512)S(1)}, f32[512]{0:T(512)}, u32[]{:S(2)}) copy-start(f32[512]{0:T(512)} %param.11) | copy-start | bytes 6148
Sparse Core Ops, SparseCore 0:
  8.9 83.4 all-gather.1
where the time goes:
time: 395 us; the launch traced here: 390 us
  matrix products  126 us (32%)
  waiting for transfers between devices  110 us (28%)
  blocking collectives  71.2 us (18%)
  local copies, waits for them, and re-layouts  35.7 us (9%)
  starting transfers between devices  22.1 us (6%)
  between operations  14.2 us (4%)
  other arithmetic  11.6 us (3%)
    all_gather x1, waiting for transfers between devices, body(): gathered = lax.all_gather(tokens, 'tp', axis=1, tiled=True)  79.9 us
    all_to_all x1, blocking collectives, inverse_transform(): lax.all_to_all(jnp.stack([back_real, back_imag]), 'ctx', split_axis=2, co...  53.4 us
    all_to_all x2, waiting for transfers between devices, body(): lax.all_to_all(values.astype(jnp.bfloat16), 'ctx', split_axis=1, concat_a...  22.4 us
    all_to_all x1, blocking collectives, inverse_transform(): lax.all_to_all(folded.reshape(row_count, width_all), 'ctx', split_axis=0,...  17.8 us
    dot_general x2, matrix products, forward_transform(): jnp.einsum('bj,ejw->ebw', inner_sin, arrived[0], precision=highest)  15.3 us
    dot_general x2, matrix products, forward_transform(): jnp.einsum('bj,ejw->ebw', inner_sin, arrived[1], precision=highest)  14.6 us
    dot_general x2, matrix products, forward_transform(): jnp.einsum('bj,ejw->ebw', inner_cos, arrived[0], precision=highest)  13.8 us
    dot_general x2, matrix products, forward_transform(): jnp.einsum('bj,ejw->ebw', inner_cos, arrived[1], precision=highest)  13.8 us
  transfers between devices with their start and end apart: 6, of which 4 were waited for; matrix products, arithmetic and copies ran while one was open for 16% of the time, Pallas kernels for 0%

commit v1 on v0

v1 whole, which is shorter than its diff:
```python
import functools
import math

import jax
import jax.numpy as jnp
import numpy as np
from jax import lax
from jax.experimental import pallas as pl
from jax.experimental.pallas import tpu as pltpu
from jax.sharding import PartitionSpec as P

highest = lax.Precision.HIGHEST


def from_behind(array, axis, by):
    devices = lax.axis_size(axis)
    pairs = [(i, i + by) for i in range(devices) if 0 <= i + by < devices]
    return lax.ppermute(array, axis, pairs)


def twist_tables(part_count, row_count):
    row = lax.optimization_barrier(jnp.arange(row_count, dtype=jnp.int32))
    turn = jnp.arange(part_count + 1, dtype=jnp.int32)[:, None] * row[None, :]
    angles = turn.astype(jnp.float32) * (math.pi / (part_count * row_count))
    return (jnp.cos(angles), jnp.sin(angles))


def inner_tables(row_count):
    row = lax.optimization_barrier(jnp.arange(row_count, dtype=jnp.int32))
    turn = row[:, None] * row[None, :] % row_count
    angles = turn.astype(jnp.float32) * (2.0 * math.pi / row_count)
    cos, sin = jnp.cos(angles), jnp.sin(angles)
    forward = jnp.block([[cos, -sin], [sin, cos]])
    backward = jnp.block([[cos, sin], [-sin, cos]])
    return lax.optimization_barrier((forward, forward.astype(jnp.bfloat16), backward.astype(jnp.bfloat16)))


def turn_of(a, k, part_count):
    step = a * k % (2 * part_count)
    cos = math.cos(math.pi * step / part_count)
    sin = math.sin(math.pi * step / part_count)
    return (0.0 if abs(cos) < 1e-12 else cos, 0.0 if abs(sin) < 1e-12 else sin)


def weighted(terms):
    total = None
    for factor, term in terms:
        if factor == 0.0:
            continue
        scaled = term if factor == 1.0 else -term if factor == -1.0 else factor * term
        total = scaled if total is None else total + scaled
    return total


def filter_spectrum(taps, part_count, twist, forward):
    channels, row_count = taps.shape[1:]
    twist_cos, twist_sin = twist
    turn = np.arange(part_count + 1)[:, None] * np.arange(part_count)[None, :] % (2 * part_count)
    outer_cos = np.cos(turn * (math.pi / part_count)).astype(np.float32)
    outer_sin = np.sin(turn * (math.pi / part_count)).astype(np.float32)
    real = jnp.einsum("ka,acm->kcm", outer_cos, taps, precision=highest)
    imag = -jnp.einsum("ka,acm->kcm", outer_sin, taps, precision=highest)
    cos, sin = twist_cos[:, None, :], twist_sin[:, None, :]
    turned = jnp.concatenate([real * cos + imag * sin, imag * cos - real * sin], axis=2)
    spectrum = jnp.einsum("kcm,mn->kcn", turned, forward, precision=highest)
    share = np.full((part_count + 1, 1, 1), 2.0, np.float32)
    share[0] = share[part_count] = 1.0
    return spectrum * (share / (2 * part_count * row_count))


def convolve_kernel(part_count, x_ref, gain_ref, cos_ref, sin_ref, forward_ref, backward_ref, y_ref, turned_ref, back_ref):
    channels, row_count = x_ref.shape[1:]
    low, high = pl.ds(0, row_count), pl.ds(row_count, row_count)
    parts = [x_ref[a].astype(jnp.float32) for a in range(part_count)]
    for k in range(part_count + 1):
        turns = [turn_of(a, k, part_count) for a in range(part_count)]
        cos, sin = cos_ref[pl.ds(k, 1), :], sin_ref[pl.ds(k, 1), :]
        real = weighted([(t[0], p) for t, p in zip(turns, parts)])
        imag = weighted([(-t[1], p) for t, p in zip(turns, parts)])
        rows = pl.ds(k * channels, channels)
        if imag is None:
            turned_ref[rows, low] = (real * cos).astype(jnp.bfloat16)
            turned_ref[rows, high] = (-real * sin).astype(jnp.bfloat16)
        else:
            turned_ref[rows, low] = (real * cos + imag * sin).astype(jnp.bfloat16)
            turned_ref[rows, high] = (imag * cos - real * sin).astype(jnp.bfloat16)
    spec = jnp.dot(turned_ref[...], forward_ref[...], preferred_element_type=jnp.float32)
    gain = gain_ref[...]
    spec_real, spec_imag = spec[:, :row_count], spec[:, row_count:]
    gain_real, gain_imag = gain[:, :row_count], gain[:, row_count:]
    turned_ref[:, low] = (spec_real * gain_real - spec_imag * gain_imag).astype(jnp.bfloat16)
    turned_ref[:, high] = (spec_real * gain_imag + spec_imag * gain_real).astype(jnp.bfloat16)
    back_ref[...] = jnp.dot(turned_ref[...], backward_ref[...], preferred_element_type=jnp.float32)
    for k in range(part_count + 1):
        cos, sin = cos_ref[pl.ds(k, 1), :], sin_ref[pl.ds(k, 1), :]
        rows = pl.ds(k * channels, channels)
        real, imag = back_ref[rows, low], back_ref[rows, high]
        back_ref[rows, low] = real * cos - imag * sin
        if 0 < k < part_count:
            back_ref[rows, high] = real * sin + imag * cos
    for a in range(part_count):
        terms = []
        for k in range(part_count + 1):
            cos, sin = turn_of(a, k, part_count)
            rows = pl.ds(k * channels, channels)
            terms.append((cos, back_ref[rows, low]))
            if sin != 0.0:
                terms.append((-sin, back_ref[rows, high]))
        y_ref[a] = weighted(terms).astype(jnp.bfloat16)


def convolve(signal, spectrum, twist, forward, backward):
    part_count, channels, row_count = signal.shape
    rows = (part_count + 1) * channels
    return pl.pallas_call(
        functools.partial(convolve_kernel, part_count),
        out_shape=jax.ShapeDtypeStruct(signal.shape, jnp.bfloat16),
        in_specs=[pl.BlockSpec(memory_space=pltpu.VMEM)] * 6,
        out_specs=pl.BlockSpec(memory_space=pltpu.VMEM),
        scratch_shapes=[
            pltpu.VMEM((rows, 2 * row_count), jnp.bfloat16),
            pltpu.VMEM((rows, 2 * row_count), jnp.float32),
        ],
        compiler_params=pltpu.CompilerParams(vmem_limit_bytes=40 << 20),
        name="convolve",
    )(
        signal,
        spectrum.reshape(rows, 2 * row_count),
        *twist,
        forward,
        backward,
    )


def body(tokens, norm_gain, proj_weight, short_taps, long_filter, skip_gain):
    part_count = lax.axis_size("ctx")
    row_count, channels = long_filter.shape
    spread = (part_count, channels // part_count, row_count)
    gathered = lax.all_gather(tokens, "tp", axis=1, tiled=True)
    taps = lax.all_to_all(long_filter.T.reshape(spread), "ctx", split_axis=0, concat_axis=0, tiled=True)
    twist = twist_tables(part_count, row_count)
    inner, forward, backward = inner_tables(row_count)
    spectrum = filter_spectrum(taps, part_count, twist, inner)
    gathered, spectrum = lax.optimization_barrier((gathered, spectrum))
    widened = gathered.astype(jnp.float32)
    scaling = lax.rsqrt(jnp.mean(widened * widened, axis=1, keepdims=True) + 1e-06)
    normed = (widened * scaling * norm_gain).astype(jnp.bfloat16)
    projected = jnp.einsum(
        "td,bdc->bct", normed, proj_weight, preferred_element_type=jnp.float32
    ).astype(jnp.bfloat16)
    previous = from_behind(projected[:, :, -2:], "ctx", 1)
    extended = jnp.concatenate([previous, projected], axis=2).astype(jnp.float32)
    branch = (
        short_taps[:, 0, :, None] * extended[:, :, 2:]
        + short_taps[:, 1, :, None] * extended[:, :, 1:-1]
        + short_taps[:, 2, :, None] * extended[:, :, :-2]
    )
    mixed = branch[1] * branch[2]
    arrived = lax.all_to_all(
        mixed.astype(jnp.bfloat16).reshape(spread), "ctx", split_axis=0, concat_axis=0, tiled=True
    )
    convolved = lax.all_to_all(
        convolve(arrived, spectrum, twist, forward, backward), "ctx", split_axis=0, concat_axis=0, tiled=True
    ).reshape(channels, row_count).astype(jnp.float32)
    return (branch[0] * (convolved + skip_gain[:, None] * mixed)).astype(jnp.bfloat16).T


def solution(mesh):
    placed = (
        P("ctx", "tp"),
        P(),
        P(None, None, "tp"),
        P(None, None, "tp"),
        P("ctx", "tp"),
        P("tp"),
    )
    return jax.shard_map(
        body, mesh=mesh, in_specs=placed, out_specs=P("ctx", "tp"), check_vma=False
    )
```

time: 395 us -> 161 us (0.41); the launches traced: 390 us -> 160 us
  matrix products: 126 us -> 23.7 us
  waiting for transfers between devices: 110 us -> 45.3 us
  blocking collectives: 71.2 us -> 28 us
  local copies, waits for them, and re-layouts: 35.7 us -> 12 us
  starting transfers between devices: 22.1 us -> 6.92 us
  other arithmetic: 11.6 us -> 26.6 us
  Pallas kernels: 0 us -> 4.23 us
    dot_general x19 -> x4, matrix products: 126 us -> 23.7 us  [the longest x1 9.89 us: body(): jnp.einsum('td,bdc->bct', normed, proj_weight, preferred_element_type=jnp...]
    all_to_all x2, blocking collectives: 71.2 us -> 28 us  [the longest x1 15.6 us: body(): lax.all_to_all(mixed.astype(jnp.bfloat16).reshape(spread), 'ctx', split_a...]
    all_gather x1, waiting for transfers between devices: 79.9 us -> 43.8 us  [body(): gathered = lax.all_gather(tokens, 'tp', axis=1, tiled=True)]
    all_to_all x4 -> x1, waiting for transfers between devices: 28.2 us -> 0.01 us  [body(): lax.all_to_all(long_filter.T.reshape(spread), 'ctx', split_axis=0, concat...]
    all_to_all x4 -> x1, starting transfers between devices: 20.4 us -> 5.17 us  [body(): lax.all_to_all(long_filter.T.reshape(spread), 'ctx', split_axis=0, concat...]
    concatenate x0 -> x3, other arithmetic: none -> 13.7 us  [the longest x1 10.7 us: inner_tables(): backward = jnp.block([[cos, sin], [-sin, cos]])]
    another operation x3 -> x0, local copies, waits for them, and re-layouts: 12.3 us -> none  [the longest x1 7.32 us: inverse_transform(): jnp.stack([back_real, back_imag])]
    slice x11 -> x2, local copies, waits for them, and re-layouts: 10.2 us -> 0.02 us  [the longest x1 0.01 us: body(): short_taps[:, 0, :, None] * extended[:, :, 2:]]
  transfers between devices with their start and end apart: 6 -> 3, of which waited for: 4 -> 2; matrix products, arithmetic and copies ran while one was open for 16% -> 22% of each run, Pallas kernels for 0% -> 0%
where the time goes in v1:
time: 161 us; the launch traced here: 160 us
  waiting for transfers between devices  45.3 us (28%)
  blocking collectives  28 us (17%)
  other arithmetic  26.6 us (17%)
  matrix products  23.7 us (15%)
  between operations  13.6 us (8%)
  local copies, waits for them, and re-layouts  12 us (7%)
  starting transfers between devices  6.92 us (4%)
  Pallas kernels  4.23 us (3%)
    all_gather x1, waiting for transfers between devices, body(): gathered = lax.all_gather(tokens, 'tp', axis=1, tiled=True)  43.8 us
    all_to_all x1, blocking collectives, body(): lax.all_to_all(mixed.astype(jnp.bfloat16).reshape(spread), 'ctx', split_a...  15.6 us
    all_to_all x1, blocking collectives, body(): lax.all_to_all(convolve(arrived, spectrum, twist, forward, backward), 'ct...  12.4 us
    concatenate x1, other arithmetic, inner_tables(): backward = jnp.block([[cos, sin], [-sin, cos]])  10.7 us
    dot_general x1, matrix products, body(): jnp.einsum('td,bdc->bct', normed, proj_weight, preferred_element_type=jnp...  9.89 us
    unnamed x27, local copies, waits for them, and re-layouts  9.2 us
    dot_general x1, matrix products, filter_spectrum(): spectrum = jnp.einsum('kcm,mn->kcn', turned, forward, precision=highest)  9.03 us
    all_to_all x1, starting transfers between devices, body(): lax.all_to_all(long_filter.T.reshape(spread), 'ctx', split_axis=0, concat...  5.17 us
  transfers between devices with their start and end apart: 3, of which 2 were waited for; matrix products, arithmetic and copies ran while one was open for 22% of the time, Pallas kernels for 0%

profile of v1, /device:TPU:0, one launch (start us, length us, event | category | flops | bytes accessed | tf_op | source)
XLA Modules:
  0.0 160.3 jit_solution(7349568735916773734)
XLA Ops:
  6.5 0.0 all-gather.2.cloned.1.call-start
  6.5 0.7 all-gather.2.cloned.1.call-update
  7.3 2.6 %copy.18 = f32[512,512]{0,1:T(8,128)} copy(f32[512,512]{1,0:T(8,128)} %param.13) | data formatting | bytes 2097152 | tf_op args[4]
  9.8 5.2 %all-to-all-start = ((f32[8,64,512]{2,1,0:T(8,128)}), f32[8,64,512]{2,1,0:T(8,128)S(1)}, u32[]{:S(2)}, u32[]{:S(2)}) async-start(f32[8,64,512]{2,1,0:T(8,128)} %bitcast.2), calls=%async_computation | async-start | bytes 2097152 | tf_op jit(solution)/shard_map/all_to_all | solution.py:140
  15.0 4.2 %fusion.37 = (bf16[512,512]{1,0:T(8,128)(2,1)S(1)}, bf16[512,512]{1,0:T(8,128)(2,1)S(1)}, bf16[512,512]{1,0:T(8,128)(2,1)S(1)}, f32[512,512]{1,0:T(8,128)S(1)}, ...) fusion(s32[512]{0:T(512)S(1)} %iota.16), kind=kLoop, calls=%fused_computation.48 | loop fusion | flops 4718592 | bytes 4720640 | tf_op jit(solution)/shard_map/convert.6
  19.3 2.4 %maximum_maximum_fusion = f32[1024,1024]{1,0:T(8,128)} fusion(f32[512,512]{1,0:T(8,128)S(1)} %get-tuple-element.27, f32[512,512]{1,0:T(8,128)S(1)} %get-tuple-element.26, f32[512,512]{1,0:T(8,128)S(1)} %get-tuple-element.25), kind=kLoop, calls=%fused_computation.8 | loop fusion | flops 3145728 | bytes 7340032 | tf_op jit(solution)/shard_map/jit(block)/concatenate | solution.py:33
  21.7 0.0 copy-start.7
  21.7 10.7 %maximum_maximum_fusion.1 = (bf16[1024,1024]{1,0:T(8,128)(2,1)}, bf16[1024,1024]{1,0:T(8,128)(2,1)}) fusion(bf16[512,512]{1,0:T(8,128)(2,1)S(1)} %get-tuple-element.23, bf16[512,512]{1,0:T(8,128)(2,1)S(1)} %get-tuple-element.24, bf16[512,512]{1,0:T(8,128)(2,1)S(1)} %get-tuple-element.22, f32[512,512]{1,0:T(8,128)S(1)} %get-tuple-element.27, ...), kind=kLoop, calls=%fused_computation.19 | loop fusion | flops 16777216 | bytes 8912896 | tf_op jit(solution)/shard_map/jit(block)/concatenate | solution.py:34
  32.4 0.0 copy-start.8
  32.4 0.0 copy-done.6
  32.4 0.1 fusion.43
  32.5 0.0 all-to-all-done
  32.5 0.0 copy-done.7
  32.5 2.2 %fusion.30 = f32[9,64,512]{2,0,1:T(8,128)S(1)} fusion(f32[9,8,1]{0,1,2:T(8,128)S(1)} %copy-done.7, f32[8,64,512]{2,1,0:T(8,128)S(1)} %all-to-all-done), kind=kOutput, calls=%fused_computation.40 | convolution fusion | flops 28311552 | bytes 2228512 | tf_op jit(solution)/shard_map/ka,acm->kcm/dot_general | solution.py:62
  34.7 0.0 copy-done.8
  34.8 2.6 %multiply_add_fusion = (f32[9,64,512]{2,0,1:T(8,128)S(1)}, f32[9,64,512]{2,0,1:T(8,128)S(1)}) fusion(f32[9,64,512]{2,0,1:T(8,128)S(1)} %fusion.30, f32[9,512]{1,0:T(8,128)S(1)} %get-tuple-element.21.sin_ref, f32[9,512]{1,0:T(8,128)S(1)} %get-tuple-element.20.cos_ref, f32[9,8,1]{0,1,2:T(8,128)S(1)} %copy-done.8, f32[8,64,512]{2,1,0:T(8,128)S(1)} %all-to-all-done), kind=kOutput, calls=%fused_computation.21 | convolution fusion | flops 30375936 | bytes 4624672 | tf_op jit(solution)/shard_map/ka,acm->kcm/dot_general | solution.py:61
  37.4 0.0 copy-start.4
  37.4 0.0 copy-start.10
  37.4 0.7 pad_maximum_fusion
  38.1 1.5 copy-done.4
  39.6 0.0 copy-done.10
  39.6 0.0 copy-start.11
  39.6 9.0 %fusion.13 = f32[9,64,1024]{2,1,0:T(8,128)S(1)} fusion(f32[1024,1024]{1,0:T(8,128)S(1)} %copy-done.4, f32[9,64,1024]{2,0,1:T(8,128)S(1)} %pad_maximum_fusion, f32[9]{0:T(128)S(1)} %copy-done.10), kind=kOutput, calls=%fused_computation.25 | convolution fusion | flops 7248347136 | bytes 8912932 | tf_op jit(solution)/shard_map/kcm,mn->kcn/dot_general | solution.py:65
  48.6 43.8 %all-gather.2.cloned.1.call-done = bf16[512,4096]{1,0:T(8,128)(2,1)} async-done(((bf16[512,1024]{1,0:T(8,128)(2,1)}), bf16[512,4096]{1,0:T(8,128)(2,1)}) %all-gather.2.cloned.1.call-update) | async-done | bytes 4194320 | tf_op jit(solution)/shard_map/all_gather | solution.py:139
  92.4 3.2 %fusion = f32[512]{0:T(512)S(1)} fusion(bf16[512,4096]{1,0:T(8,128)(2,1)} %all-gather.2.cloned.1.call-done), kind=kLoop, calls=%fused_computation.2 | loop fusion | flops 6290944 | bytes 4196352 | tf_op jit(solution)/shard_map/reduce_sum | solution.py:146
  95.7 0.0 copy-done.11
  95.7 0.2 copy-done.5
  95.9 9.9 %fusion.21 = bf16[3,512,512]{1,2,0:T(8,128)(2,1)S(1)} fusion(bf16[3,4096,512]{2,1,0:T(8,128)(2,1)} %param.11, bf16[512,4096]{1,0:T(8,128)(2,1)S(1)} %copy-done.5, f32[4096]{0:T(1024)S(1)} %copy-done.11, f32[512]{0:T(512)S(1)} %add_rsqrt_fusion), kind=kOutput, calls=%fused_computation.30 | convolution fusion | flops 6451625984 | bytes 18368512 | tf_op jit(solution)/shard_map/td,bdc->bct/dot_general | solution.py:148
  105.8 1.7 %collective-permute-start = (bf16[3,512,2]{1,2,0:T(2,128)(2,1)S(1)}, bf16[3,512,2]{1,2,0:T(2,128)(2,1)S(1)}, u32[]{:S(2)}, u32[]{:S(2)}) collective-permute-start(bf16[3,512,2]{1,2,0:T(2,128)(2,1)S(1)} %slice.40), channel_id=1, source_target_pairs={{0,4},{4,8},{8,12},{12,16},{16,20},{20,24},{24,28},{1,5},{5,9},{9,... | collective-permute-start | bytes 18440 | tf_op jit(solution)/shard_map/ppermute | solution.py:18
  107.6 0.8 collective-permute-done
  108.4 0.5 maximum_convert_fusion
  108.8 0.9 fusion.10
  109.8 0.0 copy-start.2
  109.8 1.6 %copy-done.2 = f32[3,512,512]{1,2,0:T(8,128)} copy-done((f32[3,512,512]{1,2,0:T(8,128)}, f32[3,512,512]{1,2,0:T(8,128)S(1)}, u32[]{:S(2)}) %copy-start.2) | copy-done | bytes 3145752
  111.4 0.2 fusion.41
  111.6 0.2 copy.22
  111.8 15.6 %all_to_all.15.x_ref = bf16[8,64,512]{2,1,0:T(8,128)(2,1)S(1)} all-to-all(bf16[8,64,512]{2,1,0:T(8,128)(2,1)S(1)} %bitcast.53), channel_id=1, replica_groups=mesh['ctx'=8,'tp'=4] {'ctx'}, dimensions={0} | all-to-all | bytes 1048576 | tf_op jit(solution)/shard_map/all_to_all | solution.py:159
  127.4 1.6 copy-done
  129.0 1.6 copy-done.1
  130.6 4.2 %convolve.1 = bf16[8,64,512]{2,1,0:T(8,128)(2,1)S(1)} custom-call(bf16[8,64,512]{2,1,0:T(8,128)(2,1)S(1)} %all_to_all.15.x_ref, f32[576,1024]{1,0:T(8,128)S(1)} %bitcast.52, f32[9,512]{1,0:T(8,128)S(1)} %get-tuple-element.20.cos_ref, f32[9,512]{1,0:T(8,128)S(1)} %get-tuple-element.21.sin_ref, bf16[1024,1024]{1,0:T(8,128)(2,1)S(1)} %copy-done.1, ...), custom_call_target="tpu_custom_call" | custom-call | tf_op jit(solution)/shard_map/convolve/pallas_call | solution.py:115
  134.8 0.0 copy-start.3
  134.8 0.0 copy-start.9
  134.8 12.4 %all_to_all.16 = bf16[8,64,512]{2,1,0:T(8,128)(2,1)S(1)} all-to-all(bf16[8,64,512]{2,1,0:T(8,128)(2,1)S(1)} %convolve.1), channel_id=1, replica_groups=mesh['ctx'=8,'tp'=4] {'ctx'}, dimensions={0} | all-to-all | bytes 1048576 | tf_op jit(solution)/shard_map/all_to_all | solution.py:162
  147.2 1.1 bitcast_convert_fusion
  148.4 2.5 %copy.23 = f32[512,512]{0,1:T(8,128)} copy(f32[512,512]{1,0:T(8,128)} %bitcast_convert_fusion) | data formatting | bytes 2097152 | tf_op jit(solution)/shard_map/convert_element_type | solution.py:164
  150.9 0.0 copy-done.3
  150.9 0.0 copy-done.9
  150.9 2.5 %fusion.34 = bf16[512,512]{1,0:T(8,128)(2,1)} fusion(f32[512,512]{0,1:T(8,128)} %copy.23, f32[3,512,512]{1,2,0:T(8,128)S(1)} %copy-done.3, f32[512]{0:T(512)S(1)} %copy-done.9), kind=kLoop, calls=%fused_computation.44 | loop fusion | flops 1310720 | bytes 4720640 | tf_op jit(solution)/shard_map/transpose | solution.py:165
  (10 shorter events, 0.1 us)
Async XLA Ops:
  6.5 85.9 %all-gather.2.cloned.1.call-start = ((), (), s32[]{:S(2)}) async-start(), calls=%async_computation.3 | async-start | bytes 5242880 | tf_op jit(solution)/shard_map/all_gather | solution.py:139
  9.8 22.7 %all-to-all-start = ((f32[8,64,512]{2,1,0:T(8,128)}), f32[8,64,512]{2,1,0:T(8,128)S(1)}, u32[]{:S(2)}, u32[]{:S(2)}) async-start(f32[8,64,512]{2,1,0:T(8,128)} %bitcast.2), calls=%async_computation | async-start | bytes 2097152 | tf_op jit(solution)/shard_map/all_to_all | solution.py:140
  21.7 10.7 %copy-start.6 = (f32[3,3,512]{2,1,0:T(4,128)S(1)}, f32[3,3,512]{2,1,0:T(4,128)}, u32[]{:S(2)}) copy-start(f32[3,3,512]{2,1,0:T(4,128)} %param.12) | copy-start | bytes 55300
  21.7 10.9 %copy-start.7 = (f32[9,8,1]{0,1,2:T(8,128)S(1)}, f32[9,8,1]{0,1,2:T(8,128)}, u32[]{:S(2)}) copy-start(f32[9,8,1]{0,1,2:T(8,128)} %constant.37) | copy-start | bytes 868
  32.4 2.4 %copy-start.8 = (f32[9,8,1]{0,1,2:T(8,128)S(1)}, f32[9,8,1]{0,1,2:T(8,128)}, u32[]{:S(2)}) copy-start(f32[9,8,1]{0,1,2:T(8,128)} %constant.36) | copy-start | bytes 868
  37.4 2.2 %copy-start.4 = (f32[1024,1024]{1,0:T(8,128)S(1)}, f32[1024,1024]{1,0:T(8,128)}, u32[]{:S(2)}) copy-start(f32[1024,1024]{1,0:T(8,128)} %maximum_maximum_fusion) | copy-start | bytes 12582916
  37.4 2.2 %copy-start.10 = (f32[9]{0:T(128)S(1)}, f32[9]{0:T(128)}, u32[]{:S(2)}) copy-start(f32[9]{0:T(128)} %constant.35) | copy-start | bytes 112
  39.6 56.1 %copy-start.11 = (f32[4096]{0:T(1024)S(1)}, f32[4096]{0:T(1024)}, u32[]{:S(2)}) copy-start(f32[4096]{0:T(1024)} %param.10) | copy-start | bytes 49156
  92.4 3.4 %copy-start.5 = (bf16[512,4096]{1,0:T(8,128)(2,1)S(1)}, bf16[512,4096]{1,0:T(8,128)(2,1)}, u32[]{:S(2)}) copy-start(bf16[512,4096]{1,0:T(8,128)(2,1)} %all-gather.2.cloned.1.call-done) | copy-start | bytes 12582916
  105.8 2.6 %collective-permute-start = (bf16[3,512,2]{1,2,0:T(2,128)(2,1)S(1)}, bf16[3,512,2]{1,2,0:T(2,128)(2,1)S(1)}, u32[]{:S(2)}, u32[]{:S(2)}) collective-permute-start(bf16[3,512,2]{1,2,0:T(2,128)(2,1)S(1)} %slice.40), channel_id=1, source_target_pairs={{0,4},{4,8},{8,12},{12,16},{16,20},{20,24},{24,28},{1,5},{5,9},{9,... | collective-permute-start | bytes 18440 | tf_op jit(solution)/shard_map/ppermute | solution.py:18
  109.8 1.7 %copy-start.2 = (f32[3,512,512]{1,2,0:T(8,128)}, f32[3,512,512]{1,2,0:T(8,128)S(1)}, u32[]{:S(2)}) copy-start(f32[3,512,512]{1,2,0:T(8,128)S(1)} %fusion.10) | copy-start | bytes 9437188
  127.4 1.6 copy-start
  129.0 1.6 copy-start.1
  134.8 16.1 %copy-start.3 = (f32[3,512,512]{1,2,0:T(8,128)S(1)}, f32[3,512,512]{1,2,0:T(8,128)}, u32[]{:S(2)}) copy-start(f32[3,512,512]{1,2,0:T(8,128)} %copy-done.2) | copy-start | bytes 9437188
  134.8 16.1 %copy-start.9 = (f32[512]{0:T(512)S(1)}, f32[512]{0:T(512)}, u32[]{:S(2)}) copy-start(f32[512]{0:T(512)} %param.14) | copy-start | bytes 6148
Sparse Core Ops, SparseCore 0:
  8.9 83.4 all-gather.1

commit v2 on v1

--- a/solution.py
+++ b/solution.py
@@ -68,7 +68,63 @@
     return spectrum * (share / (2 * part_count * row_count))
 
 
-def convolve_kernel(part_count, x_ref, gain_ref, cos_ref, sin_ref, forward_ref, backward_ref, y_ref, turned_ref, back_ref):
+def to_peers(part_count, me, source, target, send_sem, recv_sem):
+    copies = []
+    for shift in range(1, part_count):
+        peer = lax.rem(me + shift, part_count)
+        copies.append(
+            pltpu.make_async_remote_copy(
+                src_ref=source.at[peer],
+                dst_ref=target.at[me],
+                send_sem=send_sem.at[peer],
+                recv_sem=recv_sem.at[me],
+                device_id={"ctx": peer},
+                device_id_type=pl.DeviceIdType.MESH,
+            )
+        )
+    return copies
+
+
+def wait_for_peers(part_count, me, source, target, send_sem, recv_sem):
+    for shift in range(1, part_count):
+        peer = lax.rem(me + shift, part_count)
+        pltpu.make_async_remote_copy(
+            src_ref=source.at[peer],
+            dst_ref=target.at[peer],
+            send_sem=send_sem.at[peer],
+            recv_sem=recv_sem.at[peer],
+            device_id={"ctx": peer},
+            device_id_type=pl.DeviceIdType.MESH,
+        ).wait_recv()
+
+
+def convolve_kernel(
+    part_count, mixed_ref, gate_ref, skip_ref, cos_ref, sin_ref, gain_any, forward_any, backward_any, out_ref,
+    sent_ref, x_ref, y_ref, z_ref, gain_ref, forward_ref, backward_ref, turned_ref, back_ref,
+    local_sem, send_x, recv_x, send_y, recv_y,
+):
+    me = lax.axis_index("ctx")
+    loads = [
+        pltpu.make_async_copy(source, target, local_sem.at[i])
+        for i, (source, target) in enumerate(
+            [(forward_any, forward_ref), (gain_any, gain_ref), (backward_any, backward_ref)]
+        )
+    ]
+    for load in loads:
+        load.start()
+    barrier = pltpu.get_barrier_semaphore()
+    for shift in range(1, part_count):
+        pl.semaphore_signal(
+            barrier, inc=1, device_id={"ctx": lax.rem(me + shift, part_count)},
+            device_id_type=pl.DeviceIdType.MESH,
+        )
+    sent_ref[...] = mixed_ref[...].astype(jnp.bfloat16)
+    pl.semaphore_wait(barrier, part_count - 1)
+    out_x = to_peers(part_count, me, sent_ref, x_ref, send_x, recv_x)
+    for copy in out_x:
+        copy.start()
+    x_ref[me] = sent_ref[me]
+    wait_for_peers(part_count, me, sent_ref, x_ref, send_x, recv_x)
     channels, row_count = x_ref.shape[1:]
     low, high = pl.ds(0, row_count), pl.ds(row_count, row_count)
     parts = [x_ref[a].astype(jnp.float32) for a in range(part_count)]
@@ -84,12 +140,15 @@
         else:
             turned_ref[rows, low] = (real * cos + imag * sin).astype(jnp.bfloat16)
             turned_ref[rows, high] = (imag * cos - real * sin).astype(jnp.bfloat16)
+    loads[0].wait()
+    loads[1].wait()
     spec = jnp.dot(turned_ref[...], forward_ref[...], preferred_element_type=jnp.float32)
     gain = gain_ref[...]
     spec_real, spec_imag = spec[:, :row_count], spec[:, row_count:]
     gain_real, gain_imag = gain[:, :row_count], gain[:, row_count:]
     turned_ref[:, low] = (spec_real * gain_real - spec_imag * gain_imag).astype(jnp.bfloat16)
     turned_ref[:, high] = (spec_real * gain_imag + spec_imag * gain_real).astype(jnp.bfloat16)
+    loads[2].wait()
     back_ref[...] = jnp.dot(turned_ref[...], backward_ref[...], preferred_element_type=jnp.float32)
     for k in range(part_count + 1):
         cos, sin = cos_ref[pl.ds(k, 1), :], sin_ref[pl.ds(k, 1), :]
@@ -107,29 +166,45 @@
             if sin != 0.0:
                 terms.append((-sin, back_ref[rows, high]))
         y_ref[a] = weighted(terms).astype(jnp.bfloat16)
-
-
-def convolve(signal, spectrum, twist, forward, backward):
-    part_count, channels, row_count = signal.shape
+    out_y = to_peers(part_count, me, y_ref, z_ref, send_y, recv_y)
+    for copy in out_y:
+        copy.start()
+    z_ref[me] = y_ref[me]
+    wait_for_peers(part_count, me, y_ref, z_ref, send_y, recv_y)
+    for p in range(part_count):
+        rows = pl.ds(p * channels, channels)
+        gated = gate_ref[p] * (z_ref[p].astype(jnp.float32) + skip_ref[rows, :] * mixed_ref[p])
+        out_ref[p] = gated.astype(jnp.bfloat16)
+    for copy in out_x + out_y:
+        copy.wait_send()
+
+
+def convolve(mixed, gate, skip_gain, spectrum, twist, forward, backward):
+    part_count, channels, row_count = mixed.shape
     rows = (part_count + 1) * channels
+    held = pl.BlockSpec(memory_space=pltpu.VMEM)
+    block = (part_count, channels, row_count)
+    square = (2 * row_count, 2 * row_count)
     return pl.pallas_call(
         functools.partial(convolve_kernel, part_count),
-        out_shape=jax.ShapeDtypeStruct(signal.shape, jnp.bfloat16),
-        in_specs=[pl.BlockSpec(memory_space=pltpu.VMEM)] * 6,
-        out_specs=pl.BlockSpec(memory_space=pltpu.VMEM),
-        scratch_shapes=[
+        out_shape=jax.ShapeDtypeStruct(block, jnp.bfloat16),
+        in_specs=[held] * 5 + [pl.BlockSpec(memory_space=pl.ANY)] * 3,
+        out_specs=held,
+        scratch_shapes=[pltpu.VMEM(block, jnp.bfloat16)] * 4
+        + [
+            pltpu.VMEM((rows, 2 * row_count), jnp.float32),
+            pltpu.VMEM(square, jnp.bfloat16),
+            pltpu.VMEM(square, jnp.bfloat16),
             pltpu.VMEM((rows, 2 * row_count), jnp.bfloat16),
             pltpu.VMEM((rows, 2 * row_count), jnp.float32),
-        ],
-        compiler_params=pltpu.CompilerParams(vmem_limit_bytes=40 << 20),
+            pltpu.SemaphoreType.DMA((3,)),
+        ]
+        + [pltpu.SemaphoreType.DMA((part_count,))] * 4,
+        compiler_params=pltpu.CompilerParams(
+            vmem_limit_bytes=44 << 20, collective_id=0, has_side_effects=True
+        ),
         name="convolve",
-    )(
-        signal,
-        spectrum.reshape(rows, 2 * row_count),
-        *twist,
-        forward,
-        backward,
-    )
+    )(mixed, gate, skip_gain[:, None], *twist, spectrum.reshape(rows, 2 * row_count), forward, backward)
 
 
 def body(tokens, norm_gain, proj_weight, short_taps, long_filter, skip_gain):
@@ -156,13 +231,10 @@
         + short_taps[:, 2, :, None] * extended[:, :, :-2]
     )
     mixed = branch[1] * branch[2]
-    arrived = lax.all_to_all(
-        mixed.astype(jnp.bfloat16).reshape(spread), "ctx", split_axis=0, concat_axis=0, tiled=True
-    )
-    convolved = lax.all_to_all(
-        convolve(arrived, spectrum, twist, forward, backward), "ctx", split_axis=0, concat_axis=0, tiled=True
-    ).reshape(channels, row_count).astype(jnp.float32)
-    return (branch[0] * (convolved + skip_gain[:, None] * mixed)).astype(jnp.bfloat16).T
+    result = convolve(
+        mixed.reshape(spread), branch[0].reshape(spread), skip_gain, spectrum, twist, forward, backward
+    )
+    return result.reshape(channels, row_count).T
 
 
 def solution(mesh):

time: 161 us -> 159 us (0.988)
  blocking collectives: 28 us -> 0 us
  Pallas kernels: 4.23 us -> 24.3 us
  local copies, waits for them, and re-layouts: 12 us -> 18.7 us
    all_to_all x2 -> x0, blocking collectives: 28 us -> none  [the longest x1 15.6 us: body(): lax.all_to_all(mixed.astype(jnp.bfloat16).reshape(spread), 'ctx', split_a...]
    pallas_call x1, Pallas kernels: 4.23 us -> 24.3 us  [convolve(): pl.pallas_call(functools.partial(convolve_kernel, part_count), out_shape=...]
    convert_element_type x2 -> x0, local copies, waits for them, and re-layouts: 2.75 us -> none  [the longest x1 2.54 us: body(): convolved = lax.all_to_all(convolve(arrived, spectrum, twist, forward, ba...]
    slice x0 -> x1, local copies, waits for them, and re-layouts: none -> 2.55 us  [body(): branch[0].reshape(spread)]
    transpose x1 -> x0, other arithmetic: 2.52 us -> none  [body(): (branch[0] * (convolved + skip_gain[:, None] * mixed)).astype(jnp.bfloat16)]
    unnamed x27 -> x31, local copies, waits for them, and re-layouts: 9.2 us -> 11.7 us
    reshape x0 -> x1, local copies, waits for them, and re-layouts: none -> 2.05 us  [body(): return result.reshape(channels, row_count).T]
    slice x0 -> x1, other arithmetic: none -> 1.66 us  [body(): branch[0].reshape(spread)]
  transfers between devices with their start and end apart: 3 -> 3, of which waited for: 2 -> 1; matrix products, arithmetic and copies ran while one was open for 22% -> 22% of each run, Pallas kernels for 0% -> 0%
where the time goes in v2:
time: 159 us; the launch traced here: 158 us
  waiting for transfers between devices  44.5 us (28%)
  other arithmetic  25.8 us (16%)
  Pallas kernels  24.3 us (15%)
  matrix products  23.7 us (15%)
  local copies, waits for them, and re-layouts  18.7 us (12%)
  between operations  13.6 us (9%)
  starting transfers between devices  6.92 us (4%)
    all_gather x1, waiting for transfers between devices, body(): gathered = lax.all_gather(tokens, 'tp', axis=1, tiled=True)  43.8 us
    pallas_call x1, Pallas kernels, convolve(): pl.pallas_call(functools.partial(convolve_kernel, part_count), out_shape=...  24.3 us
    unnamed x31, local copies, waits for them, and re-layouts  11.7 us
    concatenate x1, other arithmetic, inner_tables(): backward = jnp.block([[cos, sin], [-sin, cos]])  10.7 us
    dot_general x1, matrix products, body(): jnp.einsum('td,bdc->bct', normed, proj_weight, preferred_element_type=jnp...  9.9 us
    dot_general x1, matrix products, filter_spectrum(): spectrum = jnp.einsum('kcm,mn->kcn', turned, forward, precision=highest)  9.02 us
    all_to_all x1, starting transfers between devices, body(): lax.all_to_all(long_filter.T.reshape(spread), 'ctx', split_axis=0, concat...  5.17 us
    another operation x1, other arithmetic  4.25 us
  transfers between devices with their start and end apart: 3, of which 1 were waited for; matrix products, arithmetic and copies ran while one was open for 22% of the time, Pallas kernels for 0%

profile of v2, /device:TPU:0, one launch (start us, length us, event | category | flops | bytes accessed | tf_op | source)
XLA Modules:
  0.0 157.6 jit_solution(17331378563826515038)
XLA Ops:
  6.5 0.0 all-gather.2.cloned.1.call-start
  6.5 0.7 all-gather.2.cloned.1.call-update
  7.3 2.6 %copy.21 = f32[512,512]{0,1:T(8,128)} copy(f32[512,512]{1,0:T(8,128)} %param.13) | data formatting | bytes 2097152 | tf_op args[4]
  9.9 5.2 %all-to-all-start = ((f32[8,64,512]{2,1,0:T(8,128)}), f32[8,64,512]{2,1,0:T(8,128)S(1)}, u32[]{:S(2)}, u32[]{:S(2)}) async-start(f32[8,64,512]{2,1,0:T(8,128)} %bitcast.2), calls=%async_computation | async-start | bytes 2097152 | tf_op jit(solution)/shard_map/all_to_all | solution.py:215
  15.0 4.2 %fusion.33 = (bf16[512,512]{1,0:T(8,128)(2,1)S(1)}, bf16[512,512]{1,0:T(8,128)(2,1)S(1)}, bf16[512,512]{1,0:T(8,128)(2,1)S(1)}, f32[512,512]{1,0:T(8,128)S(1)}, ...) fusion(s32[512]{0:T(512)S(1)} %iota.16), kind=kLoop, calls=%fused_computation.41 | loop fusion | flops 4718592 | bytes 4720640 | tf_op jit(solution)/shard_map/convert.5
  19.3 2.4 %maximum_maximum_fusion = f32[1024,1024]{1,0:T(8,128)} fusion(f32[512,512]{1,0:T(8,128)S(1)} %get-tuple-element.29, f32[512,512]{1,0:T(8,128)S(1)} %get-tuple-element.28, f32[512,512]{1,0:T(8,128)S(1)} %get-tuple-element.27), kind=kLoop, calls=%fused_computation.8 | loop fusion | flops 3145728 | bytes 7340032 | tf_op jit(solution)/shard_map/jit(block)/concatenate | solution.py:33
  21.7 0.0 copy-start.8
  21.7 10.7 %maximum_maximum_fusion.1 = (bf16[1024,1024]{1,0:T(8,128)(2,1)}, bf16[1024,1024]{1,0:T(8,128)(2,1)}) fusion(bf16[512,512]{1,0:T(8,128)(2,1)S(1)} %get-tuple-element.25, bf16[512,512]{1,0:T(8,128)(2,1)S(1)} %get-tuple-element.26, bf16[512,512]{1,0:T(8,128)(2,1)S(1)} %get-tuple-element.24, f32[512,512]{1,0:T(8,128)S(1)} %get-tuple-element.29, ...), kind=kLoop, calls=%fused_computation.19 | loop fusion | flops 16777216 | bytes 8912896 | tf_op jit(solution)/shard_map/jit(block)/concatenate | solution.py:34
  32.4 0.0 copy-done.8
  32.4 0.1 fusion.38
  32.5 0.0 all-to-all-done
  32.5 0.0 copy-done.9
  32.5 2.2 %fusion.27 = f32[9,64,512]{2,0,1:T(8,128)S(1)} fusion(f32[9,8,1]{0,1,2:T(8,128)S(1)} %copy-done.9, f32[8,64,512]{2,1,0:T(8,128)S(1)} %all-to-all-done), kind=kOutput, calls=%fused_computation.35 | convolution fusion | flops 28311552 | bytes 2228512 | tf_op jit(solution)/shard_map/ka,acm->kcm/dot_general | solution.py:62
  34.8 0.0 copy-done.10
  34.8 2.6 %multiply_add_fusion = (f32[9,64,512]{2,0,1:T(8,128)S(1)}, f32[9,64,512]{2,0,1:T(8,128)S(1)}) fusion(f32[9,64,512]{2,0,1:T(8,128)S(1)} %fusion.27, f32[9,512]{1,0:T(8,128)S(1)} %get-tuple-element.23.sin_ref, f32[9,512]{1,0:T(8,128)S(1)} %get-tuple-element.22.cos_ref, f32[9,8,1]{0,1,2:T(8,128)S(1)} %copy-done.10, f32[8,64,512]{2,1,0:T(8,128)S(1)} %all-to-all-done), kind=kOutput, calls=%fused_computation.21 | convolution fusion | flops 30375936 | bytes 4624672 | tf_op jit(solution)/shard_map/ka,acm->kcm/dot_general | solution.py:61
  37.4 0.0 copy-start.5
  37.4 0.0 copy-start.12
  37.4 0.7 pad_maximum_fusion
  38.1 1.5 copy-done.5
  39.6 0.0 copy-done.12
  39.6 0.0 copy-start.13
  39.6 9.0 %fusion.13 = f32[9,64,1024]{2,1,0:T(8,128)S(1)} fusion(f32[1024,1024]{1,0:T(8,128)S(1)} %copy-done.5, f32[9,64,1024]{2,0,1:T(8,128)S(1)} %pad_maximum_fusion, f32[9]{0:T(128)S(1)} %copy-done.12), kind=kOutput, calls=%fused_computation.25 | convolution fusion | flops 7248347136 | bytes 8912932 | tf_op jit(solution)/shard_map/kcm,mn->kcn/dot_general | solution.py:65
  48.7 43.8 %all-gather.2.cloned.1.call-done = bf16[512,4096]{1,0:T(8,128)(2,1)} async-done(((bf16[512,1024]{1,0:T(8,128)(2,1)}), bf16[512,4096]{1,0:T(8,128)(2,1)}) %all-gather.2.cloned.1.call-update) | async-done | bytes 4194320 | tf_op jit(solution)/shard_map/all_gather | solution.py:214
  92.4 0.0 copy-start.6
  92.4 3.2 %fusion = f32[512]{0:T(512)S(1)} fusion(bf16[512,4096]{1,0:T(8,128)(2,1)} %all-gather.2.cloned.1.call-done), kind=kLoop, calls=%fused_computation.2 | loop fusion | flops 6290944 | bytes 4196352 | tf_op jit(solution)/shard_map/reduce_sum | solution.py:221
  95.7 0.0 copy-done.13
  95.7 0.2 copy-done.6
  95.9 0.0 copy-start.11
  95.9 9.9 %fusion.21 = bf16[3,512,512]{1,2,0:T(8,128)(2,1)S(1)} fusion(bf16[3,4096,512]{2,1,0:T(8,128)(2,1)} %param.11, bf16[512,4096]{1,0:T(8,128)(2,1)S(1)} %copy-done.6, f32[4096]{0:T(1024)S(1)} %copy-done.13, f32[512]{0:T(512)S(1)} %add_rsqrt_fusion), kind=kOutput, calls=%fused_computation.30 | convolution fusion | flops 6451625984 | bytes 18368512 | tf_op jit(solution)/shard_map/td,bdc->bct/dot_general | solution.py:223
  105.8 0.0 copy-start.7
  105.8 1.1 copy-done.7
  107.0 1.7 %collective-permute-start = (bf16[3,512,2]{1,2,0:T(2,128)(2,1)S(1)}, bf16[3,512,2]{1,2,0:T(2,128)(2,1)S(1)}, u32[]{:S(2)}, u32[]{:S(2)}) collective-permute-start(bf16[3,512,2]{1,2,0:T(2,128)(2,1)S(1)} %slice.40), channel_id=1, source_target_pairs={{0,4},{4,8},{8,12},{12,16},{16,20},{20,24},{24,28},{1,5},{5,9},{9,... | collective-permute-start | bytes 18440 | tf_op jit(solution)/shard_map/ppermute | solution.py:18
  108.7 0.0 copy-done.11
  108.8 0.9 copy.27.skip_ref
  109.6 0.0 collective-permute-done
  109.6 1.9 %maximum_convert_fusion = f32[3,512,514]{1,2,0:T(8,128)S(1)} fusion(bf16[3,512,512]{1,2,0:T(8,128)(2,1)} %copy-done.7, bf16[3,512,2]{1,2,0:T(2,128)(2,1)S(1)} %collective-permute-done), kind=kLoop, calls=%fused_computation.27 | loop fusion | flops 3158016 | bytes 4737024 | tf_op jit(solution)/shard_map/convert_element_type | solution.py:227
  111.5 0.9 fusion.10
  112.4 1.7 %fusion.40 = (f32[1,512,512]{1,2,0:T(8,128)}, f32[1,512,512]{1,2,0:T(8,128)}) fusion(f32[3,512,512]{1,2,0:T(8,128)S(1)} %fusion.10), kind=kLoop, calls=%fused_computation.53 | loop fusion | flops 262144 | bytes 5242880 | tf_op jit(solution)/shard_map/slice | solution.py:235
  114.1 1.6 copy.25
  115.7 2.6 %copy.26 = f32[1,512,512]{2,1,0:T(8,128)} copy(f32[1,512,512]{1,2,0:T(8,128)} %get-tuple-element.17) | data formatting | bytes 2097152 | tf_op jit(solution)/shard_map/slice | solution.py:235
  118.2 1.6 %copy-done = bf16[1024,1024]{1,0:T(8,128)(2,1)S(1)} copy-done((bf16[1024,1024]{1,0:T(8,128)(2,1)S(1)}, bf16[1024,1024]{1,0:T(8,128)(2,1)}, u32[]{:S(2)}) %copy-start) | copy-done | bytes 2097176
  119.8 1.6 %copy-done.1 = bf16[1024,1024]{1,0:T(8,128)(2,1)S(1)} copy-done((bf16[1024,1024]{1,0:T(8,128)(2,1)S(1)}, bf16[1024,1024]{1,0:T(8,128)(2,1)}, u32[]{:S(2)}) %copy-start.1) | copy-done | bytes 2097176
  121.4 1.2 copy-done.2
  122.6 0.9 copy-done.4
  123.6 24.3 %convolve.1 = bf16[8,64,512]{2,1,0:T(8,128)(2,1)S(1)} custom-call(f32[8,64,512]{2,1,0:T(8,128)S(1)} %bitcast.36, f32[8,64,512]{2,1,0:T(8,128)S(1)} %bitcast.37, f32[512,1]{1,0:T(8,128)S(1)} %copy-done.4, f32[9,512]{1,0:T(8,128)S(1)} %get-tuple-element.22.cos_ref, f32[9,512]{1,0:T(8,128)S(1)} %get-tuple-element.23.sin_ref, f32[576,1024]{1,0:T(8,128)S(1)} %bitcast.35, ...), custom_call_target="tpu_custom_call" | custom-call | tf_op jit(solution)/shard_map/convolve/pallas_call | solution.py:188
  147.9 0.0 copy-start.3
  147.9 0.8 copy-done.3
  148.7 2.0 %copy.28 = bf16[512,512]{0,1:T(8,128)(2,1)} copy(bf16[512,512]{1,0:T(8,128)(2,1)} %bitcast.38) | data formatting | bytes 1048576 | tf_op jit(solution)/shard_map/reshape | solution.py:237
  (12 shorter events, 0.1 us)
Async XLA Ops:
  6.5 85.9 %all-gather.2.cloned.1.call-start = ((), (), s32[]{:S(2)}) async-start(), calls=%async_computation.1 | async-start | bytes 5242880 | tf_op jit(solution)/shard_map/all_gather | solution.py:214
  9.9 22.7 %all-to-all-start = ((f32[8,64,512]{2,1,0:T(8,128)}), f32[8,64,512]{2,1,0:T(8,128)S(1)}, u32[]{:S(2)}, u32[]{:S(2)}) async-start(f32[8,64,512]{2,1,0:T(8,128)} %bitcast.2), calls=%async_computation | async-start | bytes 2097152 | tf_op jit(solution)/shard_map/all_to_all | solution.py:215
  21.7 10.7 %copy-start.8 = (f32[3,3,512]{2,1,0:T(4,128)S(1)}, f32[3,3,512]{2,1,0:T(4,128)}, u32[]{:S(2)}) copy-start(f32[3,3,512]{2,1,0:T(4,128)} %param.12) | copy-start | bytes 55300
  21.7 10.9 %copy-start.9 = (f32[9,8,1]{0,1,2:T(8,128)S(1)}, f32[9,8,1]{0,1,2:T(8,128)}, u32[]{:S(2)}) copy-start(f32[9,8,1]{0,1,2:T(8,128)} %constant.37) | copy-start | bytes 868
  32.4 2.4 %copy-start.10 = (f32[9,8,1]{0,1,2:T(8,128)S(1)}, f32[9,8,1]{0,1,2:T(8,128)}, u32[]{:S(2)}) copy-start(f32[9,8,1]{0,1,2:T(8,128)} %constant.36) | copy-start | bytes 868
  37.4 2.2 %copy-start.5 = (f32[1024,1024]{1,0:T(8,128)S(1)}, f32[1024,1024]{1,0:T(8,128)}, u32[]{:S(2)}) copy-start(f32[1024,1024]{1,0:T(8,128)} %maximum_maximum_fusion) | copy-start | bytes 12582916
  37.4 2.2 %copy-start.12 = (f32[9]{0:T(128)S(1)}, f32[9]{0:T(128)}, u32[]{:S(2)}) copy-start(f32[9]{0:T(128)} %constant.35) | copy-start | bytes 112
  39.6 56.0 %copy-start.13 = (f32[4096]{0:T(1024)S(1)}, f32[4096]{0:T(1024)}, u32[]{:S(2)}) copy-start(f32[4096]{0:T(1024)} %param.10) | copy-start | bytes 49156
  92.4 3.4 %copy-start.6 = (bf16[512,4096]{1,0:T(8,128)(2,1)S(1)}, bf16[512,4096]{1,0:T(8,128)(2,1)}, u32[]{:S(2)}) copy-start(bf16[512,4096]{1,0:T(8,128)(2,1)} %all-gather.2.cloned.1.call-done) | copy-start | bytes 12582916
  95.9 12.9 %copy-start.11 = (f32[512]{0:T(512)S(1)}, f32[512]{0:T(512)}, u32[]{:S(2)}) copy-start(f32[512]{0:T(512)} %param.14) | copy-start | bytes 6148
  105.8 1.2 copy-start.7
  107.0 2.7 %collective-permute-start = (bf16[3,512,2]{1,2,0:T(2,128)(2,1)S(1)}, bf16[3,512,2]{1,2,0:T(2,128)(2,1)S(1)}, u32[]{:S(2)}, u32[]{:S(2)}) collective-permute-start(bf16[3,512,2]{1,2,0:T(2,128)(2,1)S(1)} %slice.40), channel_id=1, source_target_pairs={{0,4},{4,8},{8,12},{12,16},{16,20},{20,24},{24,28},{1,5},{5,9},{9,... | collective-permute-start | bytes 18440 | tf_op jit(solution)/shard_map/ppermute | solution.py:18
  118.2 1.6 %copy-start = (bf16[1024,1024]{1,0:T(8,128)(2,1)S(1)}, bf16[1024,1024]{1,0:T(8,128)(2,1)}, u32[]{:S(2)}) copy-start(bf16[1024,1024]{1,0:T(8,128)(2,1)} %get-tuple-element.14.backward_any) | copy-start | bytes 6291460
  119.8 1.6 %copy-start.1 = (bf16[1024,1024]{1,0:T(8,128)(2,1)S(1)}, bf16[1024,1024]{1,0:T(8,128)(2,1)}, u32[]{:S(2)}) copy-start(bf16[1024,1024]{1,0:T(8,128)(2,1)} %get-tuple-element.13.forward_any) | copy-start | bytes 6291460
  121.4 1.2 copy-start.2
  122.6 0.9 copy-start.4
  147.9 0.8 copy-start.3
Sparse Core Ops, SparseCore 0:
  8.9 83.4 all-gather.1

commit v3 on v2

--- a/solution.py
+++ b/solution.py
@@ -10,12 +10,6 @@
 from jax.sharding import PartitionSpec as P
 
 highest = lax.Precision.HIGHEST
-
-
-def from_behind(array, axis, by):
-    devices = lax.axis_size(axis)
-    pairs = [(i, i + by) for i in range(devices) if 0 <= i + by < devices]
-    return lax.ppermute(array, axis, pairs)
 
 
 def twist_tables(part_count, row_count):
@@ -99,10 +93,14 @@
 
 
 def convolve_kernel(
-    part_count, mixed_ref, gate_ref, skip_ref, cos_ref, sin_ref, gain_any, forward_any, backward_any, out_ref,
-    sent_ref, x_ref, y_ref, z_ref, gain_ref, forward_ref, backward_ref, turned_ref, back_ref,
-    local_sem, send_x, recv_x, send_y, recv_y,
+    part_count, proj_ref, taps_ref, skip_ref, cos_ref, sin_ref, gain_any, forward_any, backward_any, out_ref,
+    halo_ref, wide_ref, mixed_ref, gate_ref, sent_ref, x_ref, y_ref, z_ref, gain_ref, forward_ref,
+    backward_ref, turned_ref, back_ref, local_sem, halo_sem, send_x, recv_x, send_y, recv_y,
 ):
+    channels, row_count = x_ref.shape[1:]
+    width = proj_ref.shape[2]
+    chunk = min(width, max(128, channels))
+    blocks = chunk // channels
     me = lax.axis_index("ctx")
     loads = [
         pltpu.make_async_copy(source, target, local_sem.at[i])
@@ -118,14 +116,45 @@
             barrier, inc=1, device_id={"ctx": lax.rem(me + shift, part_count)},
             device_id_type=pl.DeviceIdType.MESH,
         )
-    sent_ref[...] = mixed_ref[...].astype(jnp.bfloat16)
+    halo = pltpu.make_async_remote_copy(
+        src_ref=proj_ref.at[:, pl.ds(row_count - 16, 16), :],
+        dst_ref=halo_ref,
+        send_sem=halo_sem.at[0],
+        recv_sem=halo_sem.at[1],
+        device_id={"ctx": lax.rem(me + 1, part_count)},
+        device_id_type=pl.DeviceIdType.MESH,
+    )
     pl.semaphore_wait(barrier, part_count - 1)
+    halo.start()
+    for i in range(3):
+        wide_ref[i, pl.ds(8, row_count), :] = proj_ref[i].astype(jnp.float32)
+    halo.wait()
+    for i in range(3):
+        before = halo_ref[i].astype(jnp.float32)[8:]
+        wide_ref[i, pl.ds(0, 8), :] = jnp.where(me > 0, before, jnp.zeros_like(before))
+
+    def branch(i, columns):
+        return (
+            taps_ref[i, pl.ds(0, 1), columns] * wide_ref[i, pl.ds(8, row_count), columns]
+            + taps_ref[i, pl.ds(1, 1), columns] * wide_ref[i, pl.ds(7, row_count), columns]
+            + taps_ref[i, pl.ds(2, 1), columns] * wide_ref[i, pl.ds(6, row_count), columns]
+        )
+
+    for j in range(width // chunk):
+        columns = pl.ds(j * chunk, chunk)
+        mixed = branch(1, columns) * branch(2, columns)
+        mixed_ref[:, columns] = mixed
+        sent_ref[pl.ds(j * blocks, blocks)] = (
+            jnp.transpose(mixed).astype(jnp.bfloat16).reshape(blocks, channels, row_count)
+        )
     out_x = to_peers(part_count, me, sent_ref, x_ref, send_x, recv_x)
     for copy in out_x:
         copy.start()
     x_ref[me] = sent_ref[me]
+    for j in range(width // chunk):
+        columns = pl.ds(j * chunk, chunk)
+        gate_ref[:, columns] = branch(0, columns)
     wait_for_peers(part_count, me, sent_ref, x_ref, send_x, recv_x)
-    channels, row_count = x_ref.shape[1:]
     low, high = pl.ds(0, row_count), pl.ds(row_count, row_count)
     parts = [x_ref[a].astype(jnp.float32) for a in range(part_count)]
     for k in range(part_count + 1):
@@ -171,26 +200,34 @@
         copy.start()
     z_ref[me] = y_ref[me]
     wait_for_peers(part_count, me, y_ref, z_ref, send_y, recv_y)
-    for p in range(part_count):
-        rows = pl.ds(p * channels, channels)
-        gated = gate_ref[p] * (z_ref[p].astype(jnp.float32) + skip_ref[rows, :] * mixed_ref[p])
-        out_ref[p] = gated.astype(jnp.bfloat16)
+    for j in range(width // chunk):
+        columns = pl.ds(j * chunk, chunk)
+        arrived = z_ref[pl.ds(j * blocks, blocks)].astype(jnp.float32).reshape(chunk, row_count)
+        direct = skip_ref[:, columns] * mixed_ref[:, columns]
+        out_ref[:, columns] = (gate_ref[:, columns] * (jnp.transpose(arrived) + direct)).astype(jnp.bfloat16)
     for copy in out_x + out_y:
         copy.wait_send()
 
 
-def convolve(mixed, gate, skip_gain, spectrum, twist, forward, backward):
-    part_count, channels, row_count = mixed.shape
+def convolve(projected, short_taps, skip_gain, spectrum, twist, forward, backward):
+    part_count, channels = spectrum.shape[0] - 1, spectrum.shape[1]
+    row_count, width = projected.shape[1:]
     rows = (part_count + 1) * channels
     held = pl.BlockSpec(memory_space=pltpu.VMEM)
     block = (part_count, channels, row_count)
     square = (2 * row_count, 2 * row_count)
     return pl.pallas_call(
         functools.partial(convolve_kernel, part_count),
-        out_shape=jax.ShapeDtypeStruct(block, jnp.bfloat16),
+        out_shape=jax.ShapeDtypeStruct((row_count, width), jnp.bfloat16),
         in_specs=[held] * 5 + [pl.BlockSpec(memory_space=pl.ANY)] * 3,
         out_specs=held,
-        scratch_shapes=[pltpu.VMEM(block, jnp.bfloat16)] * 4
+        scratch_shapes=[
+            pltpu.VMEM((3, 16, width), jnp.bfloat16),
+            pltpu.VMEM((3, row_count + 8, width), jnp.float32),
+            pltpu.VMEM((row_count, width), jnp.float32),
+            pltpu.VMEM((row_count, width), jnp.float32),
+        ]
+        + [pltpu.VMEM(block, jnp.bfloat16)] * 4
         + [
             pltpu.VMEM((rows, 2 * row_count), jnp.float32),
             pltpu.VMEM(square, jnp.bfloat16),
@@ -198,13 +235,14 @@
             pltpu.VMEM((rows, 2 * row_count), jnp.bfloat16),
             pltpu.VMEM((rows, 2 * row_count), jnp.float32),
             pltpu.SemaphoreType.DMA((3,)),
+            pltpu.SemaphoreType.DMA((2,)),
         ]
         + [pltpu.SemaphoreType.DMA((part_count,))] * 4,
         compiler_params=pltpu.CompilerParams(
-            vmem_limit_bytes=44 << 20, collective_id=0, has_side_effects=True
+            vmem_limit_bytes=56 << 20, collective_id=0, has_side_effects=True
         ),
         name="convolve",
-    )(mixed, gate, skip_gain[:, None], *twist, spectrum.reshape(rows, 2 * row_count), forward, backward)
+    )(projected, short_taps, skip_gain[None, :], *twist, spectrum.reshape(rows, 2 * row_count), forward, backward)
 
 
 def body(tokens, norm_gain, proj_weight, short_taps, long_filter, skip_gain):
@@ -221,20 +259,9 @@
     scaling = lax.rsqrt(jnp.mean(widened * widened, axis=1, keepdims=True) + 1e-06)
     normed = (widened * scaling * norm_gain).astype(jnp.bfloat16)
     projected = jnp.einsum(
-        "td,bdc->bct", normed, proj_weight, preferred_element_type=jnp.float32
+        "td,bdc->btc", normed, proj_weight, preferred_element_type=jnp.float32
     ).astype(jnp.bfloat16)
-    previous = from_behind(projected[:, :, -2:], "ctx", 1)
-    extended = jnp.concatenate([previous, projected], axis=2).astype(jnp.float32)
-    branch = (
-        short_taps[:, 0, :, None] * extended[:, :, 2:]
-        + short_taps[:, 1, :, None] * extended[:, :, 1:-1]
-        + short_taps[:, 2, :, None] * extended[:, :, :-2]
-    )
-    mixed = branch[1] * branch[2]
-    result = convolve(
-        mixed.reshape(spread), branch[0].reshape(spread), skip_gain, spectrum, twist, forward, backward
-    )
-    return result.reshape(channels, row_count).T
+    return convolve(projected, short_taps, skip_gain, spectrum, twist, forward, backward)
 
 
 def solution(mesh):

time: 159 us -> 142 us (0.89)
  local copies, waits for them, and re-layouts: 18.7 us -> 6.25 us
  other arithmetic: 25.8 us -> 21.2 us
  matrix products: 23.7 us -> 26.1 us
  starting transfers between devices: 6.92 us -> 5.17 us
  Pallas kernels: 24.3 us -> 26 us
    unnamed x31 -> x18, local copies, waits for them, and re-layouts: 11.7 us -> 6.25 us
    slice x3 -> x0, local copies, waits for them, and re-layouts: 2.58 us -> none  [the longest x1 2.55 us: body(): branch[0].reshape(spread)]
    reshape x1 -> x0, local copies, waits for them, and re-layouts: 2.05 us -> none  [body(): return result.reshape(channels, row_count).T]
    convert_element_type x1 -> x0, other arithmetic: 1.88 us -> none  [body(): jnp.concatenate([previous, projected], axis=2).astype(jnp.float32)]
    ppermute x1 -> x0, starting transfers between devices: 1.75 us -> none  [from_behind(): return lax.ppermute(array, axis, pairs)]
    pallas_call x1, Pallas kernels: 24.3 us -> 26 us  [convolve(): pl.pallas_call(functools.partial(convolve_kernel, part_count), out_shape=...]
    slice x1 -> x0, other arithmetic: 1.66 us -> none  [body(): branch[0].reshape(spread)]
  transfers between devices with their start and end apart: 3 -> 2, of which waited for: 1 -> 1; matrix products, arithmetic and copies ran while one was open for 22% -> 25% of each run, Pallas kernels for 0% -> 0%
where the time goes in v3:
time: 142 us; the launch traced here: 141 us
  waiting for transfers between devices  43.2 us (30%)
  matrix products  26.1 us (18%)
  Pallas kernels  26 us (18%)
  other arithmetic  21.2 us (15%)
  between operations  13.5 us (10%)
  local copies, waits for them, and re-layouts  6.25 us (4%)
  starting transfers between devices  5.17 us (4%)
    all_gather x1, waiting for transfers between devices, body(): gathered = lax.all_gather(tokens, 'tp', axis=1, tiled=True)  42.5 us
    pallas_call x1, Pallas kernels, convolve(): pl.pallas_call(functools.partial(convolve_kernel, part_count), out_shape=...  26 us
    dot_general x1, matrix products, body(): jnp.einsum('td,bdc->btc', normed, proj_weight, preferred_element_type=jnp...  10.8 us
    concatenate x1, other arithmetic, inner_tables(): backward = jnp.block([[cos, sin], [-sin, cos]])  10.6 us
    dot_general x1, matrix products, filter_spectrum(): spectrum = jnp.einsum('kcm,mn->kcn', turned, forward, precision=highest)  10.5 us
    unnamed x18, local copies, waits for them, and re-layouts  6.25 us
    all_to_all x1, starting transfers between devices, body(): lax.all_to_all(long_filter.T.reshape(spread), 'ctx', split_axis=0, concat...  5.17 us
    another operation x1, other arithmetic  4.25 us
  transfers between devices with their start and end apart: 2, of which 1 were waited for; matrix products, arithmetic and copies ran while one was open for 25% of the time, Pallas kernels for 0%

profile of v3, /device:TPU:0, one launch (start us, length us, event | category | flops | bytes accessed | tf_op | source)
XLA Modules:
  0.0 141.4 jit_solution(14681550830495805793)
XLA Ops:
  6.5 0.0 all-gather.2.cloned.1.call-start
  6.5 0.7 all-gather.2.cloned.1.call-update
  7.3 2.6 %copy.14 = f32[512,512]{0,1:T(8,128)} copy(f32[512,512]{1,0:T(8,128)} %param.13) | data formatting | bytes 2097152 | tf_op args[4]
  9.9 5.2 %all-to-all-start = ((f32[8,64,512]{2,1,0:T(8,128)}), f32[8,64,512]{2,1,0:T(8,128)S(1)}, u32[]{:S(2)}, u32[]{:S(2)}) async-start(f32[8,64,512]{2,1,0:T(8,128)} %bitcast.2), calls=%async_computation | async-start | bytes 2097152 | tf_op jit(solution)/shard_map/all_to_all | solution.py:253
  15.0 4.2 %fusion.31 = (bf16[512,512]{1,0:T(8,128)(2,1)S(1)}, bf16[512,512]{1,0:T(8,128)(2,1)S(1)}, bf16[512,512]{1,0:T(8,128)(2,1)S(1)}, f32[512,512]{1,0:T(8,128)S(1)}, ...) fusion(s32[512]{0:T(512)S(1)} %iota.16), kind=kLoop, calls=%fused_computation.34 | loop fusion | flops 4718592 | bytes 4720640 | tf_op jit(solution)/shard_map/convert.5
  19.3 2.3 %maximum_maximum_fusion = f32[1024,1024]{1,0:T(8,128)} fusion(f32[512,512]{1,0:T(8,128)S(1)} %get-tuple-element.24, f32[512,512]{1,0:T(8,128)S(1)} %get-tuple-element.23, f32[512,512]{1,0:T(8,128)S(1)} %get-tuple-element.22), kind=kLoop, calls=%fused_computation.8 | loop fusion | flops 3145728 | bytes 7340032 | tf_op jit(solution)/shard_map/jit(block)/concatenate | solution.py:27
  21.6 0.0 copy-start.4
  21.6 0.0 copy-start.5
  21.6 10.6 %maximum_maximum_fusion.1 = (bf16[1024,1024]{1,0:T(8,128)(2,1)}, bf16[1024,1024]{1,0:T(8,128)(2,1)}) fusion(bf16[512,512]{1,0:T(8,128)(2,1)S(1)} %get-tuple-element.20, bf16[512,512]{1,0:T(8,128)(2,1)S(1)} %get-tuple-element.21, bf16[512,512]{1,0:T(8,128)(2,1)S(1)} %get-tuple-element.19, f32[512,512]{1,0:T(8,128)S(1)} %get-tuple-element.24, ...), kind=kLoop, calls=%fused_computation.14 | loop fusion | flops 16777216 | bytes 8912896 | tf_op jit(solution)/shard_map/jit(block)/concatenate | solution.py:28
  32.2 0.1 fusion.36
  32.3 0.0 copy-start.2
  32.3 0.0 copy-start.3
  32.3 0.0 all-to-all-done
  32.4 0.0 copy-done.4
  32.4 2.2 %fusion.25 = f32[9,64,512]{2,0,1:T(8,128)S(1)} fusion(f32[9,8,1]{0,1,2:T(8,128)S(1)} %copy-done.4, f32[8,64,512]{2,1,0:T(8,128)S(1)} %all-to-all-done), kind=kOutput, calls=%fused_computation.28 | convolution fusion | flops 28311552 | bytes 2228512 | tf_op jit(solution)/shard_map/ka,acm->kcm/dot_general | solution.py:56
  34.6 0.0 copy-done.5
  34.6 2.6 %multiply_add_fusion = (f32[9,64,512]{2,0,1:T(8,128)S(1)}, f32[9,64,512]{2,0,1:T(8,128)S(1)}) fusion(f32[9,64,512]{2,0,1:T(8,128)S(1)} %fusion.25, f32[9,512]{1,0:T(8,128)S(1)} %get-tuple-element.18.sin_ref, f32[9,512]{1,0:T(8,128)S(1)} %get-tuple-element.17.cos_ref, f32[9,8,1]{0,1,2:T(8,128)S(1)} %copy-done.5, f32[8,64,512]{2,1,0:T(8,128)S(1)} %all-to-all-done), kind=kOutput, calls=%fused_computation.16 | convolution fusion | flops 30375936 | bytes 4624672 | tf_op jit(solution)/shard_map/ka,acm->kcm/dot_general | solution.py:55
  37.2 0.0 copy-done.2
  37.2 0.0 copy-done.3
  37.2 0.0 copy-start
  37.2 0.0 copy-start.6
  37.3 0.7 pad_maximum_fusion
  37.9 1.5 %copy-done = f32[1024,1024]{1,0:T(8,128)S(1)} copy-done((f32[1024,1024]{1,0:T(8,128)S(1)}, f32[1024,1024]{1,0:T(8,128)}, u32[]{:S(2)}) %copy-start) | copy-done | bytes 4194328
  39.5 0.0 copy-done.6
  39.5 0.0 copy-start.7
  39.5 10.5 %fusion.11 = f32[9,64,1024]{2,1,0:T(8,128)} fusion(f32[1024,1024]{1,0:T(8,128)S(1)} %copy-done, f32[9,64,1024]{2,0,1:T(8,128)S(1)} %pad_maximum_fusion, f32[9]{0:T(128)S(1)} %copy-done.6), kind=kOutput, calls=%fused_computation.20 | convolution fusion | flops 7248347136 | bytes 8912932 | tf_op jit(solution)/shard_map/kcm,mn->kcn/dot_general | solution.py:59
  49.9 42.5 %all-gather.2.cloned.1.call-done = bf16[512,4096]{1,0:T(8,128)(2,1)} async-done(((bf16[512,1024]{1,0:T(8,128)(2,1)}), bf16[512,4096]{1,0:T(8,128)(2,1)}) %all-gather.2.cloned.1.call-update) | async-done | bytes 4194320 | tf_op jit(solution)/shard_map/all_gather | solution.py:252
  92.4 0.0 copy-start.1
  92.4 3.2 %fusion = f32[512]{0:T(512)S(1)} fusion(bf16[512,4096]{1,0:T(8,128)(2,1)} %all-gather.2.cloned.1.call-done), kind=kLoop, calls=%fused_computation.2 | loop fusion | flops 6290944 | bytes 4196352 | tf_op jit(solution)/shard_map/reduce_sum | solution.py:259
  95.7 0.0 copy-done.7
  95.7 0.2 copy-done.1
  95.9 10.8 %fusion.19.proj_ref = bf16[3,512,512]{2,1,0:T(8,128)(2,1)} fusion(bf16[3,4096,512]{2,1,0:T(8,128)(2,1)} %param.11, bf16[512,4096]{1,0:T(8,128)(2,1)S(1)} %copy-done.1, f32[4096]{0:T(1024)S(1)} %copy-done.7, f32[512]{0:T(512)S(1)} %add_rsqrt_fusion), kind=kOutput, calls=%fused_computation.24 | convolution fusion | flops 6451625984 | bytes 18368512 | tf_op jit(solution)/shard_map/td,bdc->btc/dot_general | solution.py:261
  106.7 26.0 %convolve.1 = bf16[512,512]{1,0:T(8,128)(2,1)} custom-call(bf16[3,512,512]{2,1,0:T(8,128)(2,1)} %fusion.19.proj_ref, f32[3,3,512]{2,1,0:T(4,128)} %taps_ref.1, f32[1,512]{1,0:T(1,128)} %bitcast.25, f32[9,512]{1,0:T(8,128)} %copy-done.2, f32[9,512]{1,0:T(8,128)} %copy-done.3, f32[576,1024]{1,0:T(8,128)} %bitcast.24, ...), custom_call_target="tpu_custom_call" | custom-call | tf_op jit(solution)/shard_map/convolve/pallas_call | solution.py:219
  132.7 1.9 %copy.29 = bf16[512,512]{1,0:T(8,128)(2,1)} copy(bf16[512,512]{1,0:T(8,128)(2,1)} %convolve.1) | data formatting | bytes 1048576
  (2 shorter events, 0.0 us)
Async XLA Ops:
  6.5 85.9 %all-gather.2.cloned.1.call-start = ((), (), s32[]{:S(2)}) async-start(), calls=%async_computation.1 | async-start | bytes 5242880 | tf_op jit(solution)/shard_map/all_gather | solution.py:252
  9.9 22.5 %all-to-all-start = ((f32[8,64,512]{2,1,0:T(8,128)}), f32[8,64,512]{2,1,0:T(8,128)S(1)}, u32[]{:S(2)}, u32[]{:S(2)}) async-start(f32[8,64,512]{2,1,0:T(8,128)} %bitcast.2), calls=%async_computation | async-start | bytes 2097152 | tf_op jit(solution)/shard_map/all_to_all | solution.py:253
  21.6 10.8 %copy-start.4 = (f32[9,8,1]{0,1,2:T(8,128)S(1)}, f32[9,8,1]{0,1,2:T(8,128)}, u32[]{:S(2)}) copy-start(f32[9,8,1]{0,1,2:T(8,128)} %constant.37) | copy-start | bytes 868
  21.6 13.0 %copy-start.5 = (f32[9,8,1]{0,1,2:T(8,128)S(1)}, f32[9,8,1]{0,1,2:T(8,128)}, u32[]{:S(2)}) copy-start(f32[9,8,1]{0,1,2:T(8,128)} %constant.36) | copy-start | bytes 868
  32.3 4.9 %copy-start.2 = (f32[9,512]{1,0:T(8,128)}, f32[9,512]{1,0:T(8,128)S(1)}, u32[]{:S(2)}) copy-start(f32[9,512]{1,0:T(8,128)S(1)} %get-tuple-element.17.cos_ref) | copy-start | bytes 55300
  32.3 4.9 %copy-start.3 = (f32[9,512]{1,0:T(8,128)}, f32[9,512]{1,0:T(8,128)S(1)}, u32[]{:S(2)}) copy-start(f32[9,512]{1,0:T(8,128)S(1)} %get-tuple-element.18.sin_ref) | copy-start | bytes 55300
  37.2 2.2 %copy-start = (f32[1024,1024]{1,0:T(8,128)S(1)}, f32[1024,1024]{1,0:T(8,128)}, u32[]{:S(2)}) copy-start(f32[1024,1024]{1,0:T(8,128)} %maximum_maximum_fusion) | copy-start | bytes 12582916
  37.2 2.2 %copy-start.6 = (f32[9]{0:T(128)S(1)}, f32[9]{0:T(128)}, u32[]{:S(2)}) copy-start(f32[9]{0:T(128)} %constant.35) | copy-start | bytes 112
  39.5 56.2 %copy-start.7 = (f32[4096]{0:T(1024)S(1)}, f32[4096]{0:T(1024)}, u32[]{:S(2)}) copy-start(f32[4096]{0:T(1024)} %param.10) | copy-start | bytes 49156
  92.4 3.4 %copy-start.1 = (bf16[512,4096]{1,0:T(8,128)(2,1)S(1)}, bf16[512,4096]{1,0:T(8,128)(2,1)}, u32[]{:S(2)}) copy-start(bf16[512,4096]{1,0:T(8,128)(2,1)} %all-gather.2.cloned.1.call-done) | copy-start | bytes 12582916
Sparse Core Ops, SparseCore 0:
  8.9 83.4 all-gather.1
